TPU v7x, 32 devices: a whole 2x2x4 slice. The times are simulated.
32 devices in a mesh: ep: 8 (over z, x), tp: 4 (over y, core).
Axes of the slice: x: 2, y: 2, z: 4, core: 2. Of those that a mesh axis runs over, the one named last changes fastest.
Arguments:
- hidden_in: bfloat16 [2048, 3584], P('ep', 'tp'), may hold values from -6 to 6
- moe_gain: bfloat16 [3584], replicated, may hold values from 0.099609375 to 1.8984375
- router_weight: bfloat16 [3584, 256], P('tp'), may hold values from -0.09375 to 0.09375
- expert_ids: int32 [2048, 8], P('ep'), may hold values from 0 to 255, all different within a row; in each aligned block of 256 rows (0 to 255, 256 to 511, ...) at most 16 rows name the same one
- shared_gate: bfloat16 [3584, 1024], P(None, 'tp'), may hold values from -0.09375 to 0.09375
- shared_up: bfloat16 [3584, 1024], P(None, 'tp'), may hold values from -0.09375 to 0.09375
- shared_down: bfloat16 [1024, 3584], P('tp'), may hold values from -0.1875 to 0.1875
- expert_gate: bfloat16 [8, 3584, 1024], P('ep', None, 'tp'), may hold values from -0.09375 to 0.09375
- expert_up: bfloat16 [8, 3584, 1024], P('ep', None, 'tp'), may hold values from -0.09375 to 0.09375
- expert_down: bfloat16 [8, 1024, 3584], P('ep', 'tp'), may hold values from -0.1875 to 0.1875
- attn_gain: bfloat16 [3584], P('tp'), may hold values from 0.099609375 to 1.8984375
- kv_down: bfloat16 [3584, 576], P('tp'), may hold values from -0.09375 to 0.09375
- kv_gain: bfloat16 [512], replicated, may hold values from 0.099609375 to 1.8984375
- doc_lengths: int32 [8, 4], P('ep'), may hold values from 1 to 128, 256 in all within a row
- page_table: int32 [8, 4], P('ep'), may hold values from 0 to 3, each once within a row
Outputs:
- layer_out: bfloat16 [2048, 3584], P('ep', 'tp')
- kv_pages: bfloat16 [8, 4, 64, 576], P('ep', 'tp')
Inputs may be any that keep to these rules, and one draw needn't show every extreme that they name: `expert_ids`: each row names 8 different experts. Among the rows of one ep index no expert is named more than 16 times. `doc_lengths`: each row sums to 256. `page_table`: each row holds every number below 4 once.
All inputs are finite; a program needn't handle non-finite values.
Results may differ from a plain program's by a relative error of at most 0.0065.
Values may be sent and summed in bfloat16 or wider, within the bound.
No kernel may reach another device: no remote copies, remote signals or barrier semaphores. Data moves between devices by JAX's collectives and lax.ppermute only.
A program may use at most 128 MiB of HBM per device.

v0:
```python
import jax
import jax.numpy as jnp
from jax import lax
from jax.sharding import PartitionSpec as P

CAP = 16
KVR = 512


EPS = 1e-06
ROUTE_SCALE = 2.5
THETA = 10000.0


def silu(values):
    return values / (1.0 + jnp.exp(-values))


def route_weights(logits, expert_ids):
    scores = 1.0 / (1.0 + jnp.exp(-logits))
    picked = jnp.take_along_axis(scores, expert_ids, axis=1)
    return ROUTE_SCALE * picked / jnp.sum(picked, axis=1, keepdims=True)


def slot_table(expert_ids, gate_weights, expert_count, capacity):
    token_count = expert_ids.shape[0]
    columns = jnp.arange(expert_count, dtype=jnp.int32)
    matched = expert_ids[:, :, None] == columns[None, None, :]
    weight_rows = jnp.sum(jnp.where(matched, gate_weights[:, :, None], 0.0), axis=1)
    chosen = jnp.any(matched, axis=1).astype(jnp.int32)
    before = jnp.cumsum(chosen, axis=0) - chosen
    target = jnp.where(chosen > 0, columns[None, :] * capacity + before, expert_count * capacity)
    token_index = jnp.broadcast_to(jnp.arange(token_count, dtype=jnp.int32)[:, None], target.shape)
    slot_token = (
        jnp.full((expert_count * capacity + 1,), token_count, jnp.int32)
        .at[target.reshape(-1)]
        .set(token_index.reshape(-1))
    )
    slot_weight = (
        jnp.zeros((expert_count * capacity + 1,), jnp.float32)
        .at[target.reshape(-1)]
        .set(weight_rows.reshape(-1))
    )
    return (slot_token[:-1], slot_weight[:-1])


def positions_of(lengths, token_count):
    doc_ends = jnp.cumsum(lengths)
    doc_starts = doc_ends - lengths
    token_index = jnp.arange(token_count, dtype=jnp.int32)
    doc_begin = jnp.max(
        jnp.where(doc_starts[None, :] <= token_index[:, None], doc_starts[None, :], 0), axis=1
    )
    return (token_index - doc_begin).astype(jnp.float32)


def rotate(rope_part, position):
    half_width = rope_part.shape[1] // 2
    frequency = THETA ** (-jnp.arange(half_width, dtype=jnp.float32) * 2.0 / rope_part.shape[1])
    angles = position[:, None] * frequency[None, :]
    cosine = jnp.cos(angles)
    sine_part = jnp.sin(angles)
    first_half = rope_part[:, :half_width]
    second_half = rope_part[:, half_width:]
    return jnp.concatenate(
        [
            first_half * cosine - second_half * sine_part,
            second_half * cosine + first_half * sine_part,
        ],
        axis=1,
    )


def finish(latent, position, kv_gain):
    plain_part = latent[:, :KVR]
    row_scale = lax.rsqrt(jnp.mean(plain_part * plain_part, axis=1, keepdims=True) + EPS)
    normed = plain_part * row_scale * kv_gain.astype(jnp.float32)
    return jnp.concatenate([normed, rotate(latent[:, KVR:], position)], axis=1).astype(jnp.bfloat16)


def per_device(
    hidden_in,
    moe_gain,
    router_weight,
    expert_ids,
    shared_gate,
    shared_up,
    shared_down,
    expert_gate,
    expert_up,
    expert_down,
    attn_gain,
    kv_down,
    kv_gain,
    doc_lengths,
    page_table,
):
    groups = lax.axis_size("ep")
    tp_count = lax.axis_size("tp")
    member = lax.axis_index("tp")
    tok_rows, width_local = hidden_in.shape
    full_width = width_local * tp_count
    capacity = CAP
    gathered = lax.all_gather(hidden_in, "tp", axis=1, tiled=True)
    stream = gathered.astype(jnp.float32)
    inverse = lax.rsqrt(jnp.mean(stream * stream, axis=1, keepdims=True) + EPS)
    normed = (stream * inverse * moe_gain.astype(jnp.float32)).astype(jnp.bfloat16)
    normed_local = lax.dynamic_slice_in_dim(normed, member * width_local, width_local, 1)
    logits = lax.psum(
        jnp.dot(normed_local, router_weight, preferred_element_type=jnp.float32).astype(
            jnp.bfloat16
        ),
        "tp",
    ).astype(jnp.float32)
    gate_weights = route_weights(logits, expert_ids)
    slot_token, slot_weight = slot_table(expert_ids, gate_weights, groups, capacity)
    shared_hidden = (
        silu(jnp.dot(normed, shared_gate, preferred_element_type=jnp.float32))
        * jnp.dot(normed, shared_up, preferred_element_type=jnp.float32)
    ).astype(jnp.bfloat16)
    shared_part = jnp.dot(shared_hidden, shared_down, preferred_element_type=jnp.float32)
    w_gate = expert_gate[0]
    w_up = expert_up[0]
    w_down = expert_down[0]
    padded = jnp.concatenate([normed, jnp.zeros((1, full_width), jnp.bfloat16)], axis=0)
    send_rows = padded[slot_token].reshape(groups, capacity, full_width)
    arrived_block = lax.all_to_all(send_rows, "ep", split_axis=0, concat_axis=0, tiled=True)
    flat_rows = arrived_block.reshape(-1, full_width)
    hidden_rows = (
        silu(jnp.dot(flat_rows, w_gate, preferred_element_type=jnp.float32))
        * jnp.dot(flat_rows, w_up, preferred_element_type=jnp.float32)
    ).astype(jnp.bfloat16)
    result = jnp.dot(hidden_rows, w_down, preferred_element_type=jnp.float32)
    outputs = result.reshape(arrived_block.shape[0], arrived_block.shape[1], full_width)
    reduced = lax.psum_scatter(outputs, "tp", scatter_dimension=2, tiled=True)
    returned = lax.all_to_all(reduced, "ep", split_axis=0, concat_axis=0, tiled=True)
    weighted = returned.reshape(groups * capacity, width_local) * slot_weight[:, None]
    routed = jax.ops.segment_sum(weighted, slot_token, num_segments=tok_rows + 1)[:tok_rows]
    branch_sum = lax.psum_scatter(shared_part, "tp", scatter_dimension=1, tiled=True) + routed
    layer_out = (hidden_in.astype(jnp.float32) + branch_sum).astype(jnp.bfloat16)
    out_values = layer_out.astype(jnp.float32)
    scaled = (out_values * attn_gain.astype(jnp.float32)).astype(jnp.bfloat16)
    latent_part = jnp.dot(scaled, kv_down, preferred_element_type=jnp.float32)
    squares = jnp.sum(out_values * out_values, axis=1)
    positions = positions_of(doc_lengths[0], tok_rows)
    page_count = page_table.shape[1]
    per_owner = page_count // tp_count
    page_len = tok_rows // page_count
    own_slots = lax.dynamic_slice_in_dim(page_table[0], member * per_owner, per_owner, 0)
    latent_sum, energy = lax.psum((latent_part, squares), "tp")
    latent = latent_sum * lax.rsqrt(energy / full_width + EPS)[:, None]
    row_index = (
        own_slots[:, None] * page_len + jnp.arange(page_len, dtype=jnp.int32)[None, :]
    ).reshape(-1)
    cache_rows = finish(latent[row_index], positions[row_index], kv_gain)
    page_out = cache_rows.reshape(1, per_owner, page_len, cache_rows.shape[-1])
    return (layer_out, page_out)


def solution(mesh):
    placed = (
        P("ep", "tp"),
        P(),
        P("tp", None),
        P("ep", None),
        P(None, "tp"),
        P(None, "tp"),
        P("tp", None),
        P("ep", None, "tp"),
        P("ep", None, "tp"),
        P("ep", "tp", None),
        P("tp"),
        P("tp", None),
        P(),
        P("ep", None),
        P("ep", None),
    )
    return jax.shard_map(
        per_device,
        mesh=mesh,
        in_specs=placed,
        out_specs=(P("ep", "tp"), P("ep", "tp", None, None)),
        check_vma=False,
    )
```

profile of v0, /device:TPU:0, one launch (start us, length us, event | category | flops | bytes accessed | tf_op | source)
XLA Modules:
  0.0 229.4 jit_solution(17543167574252839877)
XLA Ops:
  7.2 0.0 all-gather.2.cloned.1.call-start
  7.2 0.7 all-gather.2.cloned.1.call-update
  7.9 0.0 reduce-scatter.5.cloned.1.call-start
  8.0 0.7 fusion.33
  8.7 0.6 reduce-window.9
  9.3 0.2 slice_reduce_fusion
  9.5 0.7 convert_element_type.59
  10.2 0.1 fusion.45
  10.3 0.1 copy.34
  10.5 0.1 reshape.197
  10.6 0.1 reshape.239
  10.7 8.0 %scatter_custom_fusion = s32[129]{0:T(256)S(1)} fusion(s32[2048]{0:T(1024)S(1)} %bitcast.59, s32[2048]{0:T(1024)S(1)} %reshape.239, s32[]{:T(128)} %constant.28.clone.1), kind=kCustom, calls=%fused_computation.93 | custom fusion | bytes 520 | tf_op jit(solution)/shard_map/scatter | solution.py:37
  18.8 14.7 %all-gather.2.cloned.1.call-done = bf16[256,3584]{1,0:T(8,128)(2,1)} async-done(((bf16[256,896]{1,0:T(8,128)(2,1)}), bf16[256,3584]{1,0:T(8,128)(2,1)}) %all-gather.2.cloned.1.call-update) | async-done | bytes 1835024 | tf_op jit(solution)/shard_map/all_gather | solution.py:104
  33.4 2.1 fusion
  35.5 0.5 fusion.2
  36.1 1.2 copy-done.1
  37.3 1.4 concatenate.20
  38.7 3.8 %gather_fusion = bf16[128,3584]{1,0:T(8,128)(2,1)S(1)} fusion(bf16[257,3584]{1,0:T(8,128)(2,1)} %concatenate.20, s32[1024]{0:T(1024)S(1)} %pad_clamp_fusion.1), kind=kCustom, calls=%fused_computation | custom fusion | bytes 1835520 | tf_op jit(solution)/shard_map/gather | solution.py:126
  42.5 29.1 %all_to_all.10 = bf16[8,16,3584]{2,1,0:T(8,128)(2,1)S(1)} all-to-all(bf16[8,16,3584]{2,1,0:T(8,128)(2,1)S(1)} %bitcast.57), channel_id=1, replica_groups=mesh['ep'=8,'tp'=4] {'ep'}, dimensions={0} | all-to-all | bytes 1835008 | tf_op jit(solution)/shard_map/all_to_all | solution.py:127
  71.7 0.4 fusion.7
  72.1 1.1 copy-done.6
  73.2 0.4 fusion.14
  73.6 1.1 copy-done.3
  74.7 1.7 fusion.3
  76.4 0.0 all-reduce.4.cloned.1.call-start
  76.4 0.9 copy-done.9
  77.4 2.0 convolution_convert_fusion
  79.4 2.8 %fusion.56 = f32[256,256]{1,0:T(8,128)S(1)} fusion(bf16[256,3584]{1,0:T(8,128)(2,1)} %copy-done.1, bf16[3584,256]{1,0:T(8,128)(2,1)} %param.19), kind=kOutput, calls=%fused_computation.97 | convolution fusion | flops 469762048 | bytes 3932160 | tf_op jit(solution)/shard_map/dot_general | solution.py:118
  82.2 0.0 reduce-scatter.3.cloned.1.call-start
  82.2 6.1 %fusion.13 = f32[256,3584]{1,0:T(8,128)} fusion(bf16[256,3584]{1,0:T(8,128)(2,1)S(1)} %copy-done, bf16[256,3584]{1,0:T(8,128)(2,1)} %copy-done.1, bf16[3584,256]{1,0:T(8,128)(2,1)} %param.20, f32[256,256]{1,0:T(8,128)S(1)} %fusion.56), kind=kOutput, calls=%fused_computation.24 | convolution fusion | flops 939851776 | bytes 9437184 | tf_op jit(solution)/shard_map/dot_general | solution.py:121
  88.4 0.6 copy-done.14
  89.0 0.2 reduce-window_2_clone.1
  89.2 0.6 fusion.55
  89.7 0.1 select_reduce_fusion.1
  89.9 14.1 %reduce-scatter.5.cloned.1.call-done = f32[8,16,896]{2,1,0:T(8,128)} async-done(((f32[8,16,3584]{2,1,0:T(8,128)}), f32[8,16,896]{2,1,0:T(8,128)}) %reduce-scatter.5.cloned.1.call-update) | async-done | bytes 458768 | tf_op jit(solution)/shard_map/reduce_scatter | solution.py:135
  103.9 5.5 %all-to-all-start.1 = ((f32[8,16,896]{2,1,0:T(8,128)}), f32[8,16,896]{2,1,0:T(8,128)S(1)}, u32[]{:S(2)}, u32[]{:S(2)}) async-start(f32[8,16,896]{2,1,0:T(8,128)} %reduce-scatter.5.cloned.1.call-done), calls=%async_computation.3 | async-start | bytes 917504 | tf_op jit(solution)/shard_map/all_to_all | solution.py:136
  109.4 0.0 all-reduce.6.cloned.1.call-start
  109.5 0.7 fusion.47
  110.2 0.1 copy.35
  110.3 0.1 reshape.229
  110.4 0.8 gather_fusion.2
  111.2 27.4 %all-reduce.4.cloned.1.call-done = bf16[256,256]{1,0:T(8,128)(2,1)} async-done(((bf16[256,256]{1,0:T(8,128)(2,1)}), bf16[256,256]{1,0:T(8,128)(2,1)}) %all-reduce.4.cloned.1.call-update) | async-done | bytes 131088 | tf_op jit(solution)/shard_map/psum | solution.py:109
  138.6 1.0 add_divide_fusion
  139.6 16.6 %gather_fusion.3 = f32[2048]{0:T(1024)S(1)} fusion(f32[256,256]{1,0:T(8,128)S(1)} %add_divide_fusion, s32[2048]{0:T(1024)S(1)} %reshape.229), kind=kCustom, calls=%fused_computation.3 | custom fusion | bytes 32768 | tf_op jit(solution)/shard_map/jit(take_along_axis)/gather | solution.py:21
  156.2 0.1 reshape.232
  156.4 0.1 copy.36
  156.5 0.1 copy.37
  156.6 0.1 reshape.247
  156.7 8.0 %scatter_custom_fusion.1 = f32[129]{0:T(256)S(1)} fusion(s32[2048]{0:T(1024)S(1)} %bitcast.60, f32[2048]{0:T(1024)S(1)} %reshape.247, f32[]{:T(128)} %constant.24.clone.1), kind=kCustom, calls=%fused_computation.88 | custom fusion | bytes 520 | tf_op jit(solution)/shard_map/scatter | solution.py:42
  164.8 0.9 bitcast_multiply_fusion
  165.7 2.3 %scatter_custom_fusion.2 = f32[257,896]{1,0:T(8,128)S(1)} fusion(s32[128]{0:T(128)S(1)} %get-tuple-element.7, f32[128,896]{1,0:T(8,128)} %bitcast_multiply_fusion, f32[]{:T(128)} %constant.24.clone.1), kind=kCustom, calls=%fused_computation.31 | custom fusion | flops 114688 | bytes 921600 | tf_op jit(solution)/shard_map/scatter-add | solution.py:138
  168.0 14.1 %reduce-scatter.3.cloned.1.call-done = f32[256,896]{1,0:T(8,128)} async-done(((f32[256,3584]{1,0:T(8,128)}), f32[256,896]{1,0:T(8,128)}) %reduce-scatter.3.cloned.1.call-update) | async-done | bytes 917520 | tf_op jit(solution)/shard_map/reduce_scatter | solution.py:139
  182.1 1.5 fusion.18
  183.7 0.8 copy-done.7
  184.4 1.3 fusion.23
  185.8 5.8 %psum.23 = f32[256]{0:T(256)S(1)} all-reduce(f32[256]{0:T(256)S(1)} %get-tuple-element.2), channel_id=1, replica_groups=mesh['ep'=8,'tp'=4] {'tp'}, use_global_device_ids=true, to_apply=%region_14.15 | all-reduce | flops 256 | bytes 2048 | tf_op jit(solution)/shard_map/psum | solution.py:150
  191.6 28.2 %all-reduce.6.cloned.1.call-done = f32[256,576]{0,1:T(8,128)} async-done(((f32[256,576]{0,1:T(8,128)}), f32[256,576]{0,1:T(8,128)}) %all-reduce.6.cloned.1.call-update) | async-done | bytes 589840 | tf_op jit(solution)/shard_map/psum | solution.py:150
  219.7 1.1 broadcast_multiply_fusion
  220.8 0.2 copy.38
  221.1 0.7 gather_fusion.1
  221.8 0.1 multiply_reduce_fusion
  221.9 0.2 fusion.43
  222.1 0.1 fusion.32
  222.2 0.7 pad_maximum_fusion
  (51 shorter events, 0.3 us)
Async XLA Ops:
  7.2 75.1 %copy-start = (bf16[256,3584]{1,0:T(8,128)(2,1)S(1)}, bf16[256,3584]{1,0:T(8,128)(2,1)}, u32[]{:S(2)}) copy-start(bf16[256,3584]{1,0:T(8,128)(2,1)} %param.21) | copy-start | bytes 5505028
  7.2 26.3 %all-gather.2.cloned.1.call-start = ((), (), s32[]{:S(2)}) async-start(), calls=%async_computation.4 | async-start | bytes 2293760 | tf_op jit(solution)/shard_map/all_gather | solution.py:104
  7.9 96.0 %reduce-scatter.5.cloned.1.call-start = ((), (), s32[]{:S(2)}) async-start(), calls=%async_computation.6 | async-start | bytes 2293760 | tf_op jit(solution)/shard_map/reduce_scatter | solution.py:135
  33.4 2.1 copy-start.2
  36.1 1.3 copy-start.1
  42.5 29.1 %copy-start.5 = (bf16[1,3584,256]{2,1,0:T(8,128)(2,1)S(1)}, bf16[1,3584,256]{2,1,0:T(8,128)(2,1)}, u32[]{:S(2)}) copy-start(bf16[1,3584,256]{2,1,0:T(8,128)(2,1)} %param.22) | copy-start | bytes 5505028
  71.7 1.5 copy-start.6
  73.2 1.5 copy-start.3
  76.4 1.0 copy-start.9
  76.4 62.2 %all-reduce.4.cloned.1.call-start = ((), (), s32[]{:S(2)}) async-start(), calls=%async_computation.7 | async-start | bytes 262144 | tf_op jit(solution)/shard_map/psum | solution.py:109
  82.2 99.9 %reduce-scatter.3.cloned.1.call-start = ((), (), s32[]{:S(2)}) async-start(), calls=%async_computation.5 | async-start | bytes 4587520 | tf_op jit(solution)/shard_map/reduce_scatter | solution.py:139
  88.3 0.7 copy-start.14
  88.3 0.8 copy-start.13
  88.3 1.5 copy-start.10
  88.3 21.8 %copy-start.12 = (bf16[512]{0:T(512)(128)(2,1)S(1)}, bf16[512]{0:T(512)(128)(2,1)}, u32[]{:S(2)}) copy-start(bf16[512]{0:T(512)(128)(2,1)} %param.27) | copy-start | bytes 3076
  88.3 21.8 %copy-start.11 = (bf16[896]{0:T(1024)(128)(2,1)S(1)}, bf16[896]{0:T(1024)(128)(2,1)}, u32[]{:S(2)}) copy-start(bf16[896]{0:T(1024)(128)(2,1)} %param.25) | copy-start | bytes 5380
  103.9 60.9 %all-to-all-start.1 = ((f32[8,16,896]{2,1,0:T(8,128)}), f32[8,16,896]{2,1,0:T(8,128)S(1)}, u32[]{:S(2)}, u32[]{:S(2)}) async-start(f32[8,16,896]{2,1,0:T(8,128)} %reduce-scatter.5.cloned.1.call-done), calls=%async_computation.3 | async-start | bytes 917504 | tf_op jit(solution)/shard_map/all_to_all | solution.py:136
  109.4 110.3 %all-reduce.6.cloned.1.call-start = ((), (), s32[]{:S(2)}) async-start(), calls=%async_computation.8 | async-start | bytes 1179648 | tf_op jit(solution)/shard_map/psum | solution.py:150
  156.2 25.9 %copy-start.4 = (bf16[256,896]{1,0:T(8,128)(2,1)S(1)}, bf16[256,896]{1,0:T(8,128)(2,1)}, u32[]{:S(2)}) copy-start(bf16[256,896]{1,0:T(8,128)(2,1)} %param.15) | copy-start | bytes 1376260
  182.1 2.3 %copy-start.8 = (bf16[896,576]{0,1:T(8,128)(2,1)S(1)}, bf16[896,576]{0,1:T(8,128)(2,1)}, u32[]{:S(2)}) copy-start(bf16[896,576]{0,1:T(8,128)(2,1)} %param.26) | copy-start | bytes 3096580
  183.7 0.8 copy-start.7
Sparse Core Ops, SparseCore 0:
  9.6 23.8 all-gather.1
  76.5 27.3 reduce-scatter.4
  106.8 31.7 all-reduce.3
  141.0 41.0 reduce-scatter.2
  185.9 33.7 all-reduce.5
where the time goes:
time: 230 us; the launch traced here: 229 us
  waiting for transfers between devices  99.2 us (43%)
  local copies, waits for them, and re-layouts  46.6 us (20%)
  blocking collectives  34.9 us (15%)
  matrix products  14.7 us (6%)
  other arithmetic  14.3 us (6%)
  between operations  14.1 us (6%)
  starting transfers between devices  5.7 us (2%)
    all_to_all x1, blocking collectives, per_device(): lax.all_to_all(send_rows, 'ep', split_axis=0, concat_axis=0, tiled=True)  29.1 us
    psum x1, waiting for transfers between devices, per_device(): latent_sum, energy = lax.psum((latent_part, squares), 'tp')  28.2 us
    psum x1, waiting for transfers between devices, per_device(): lax.psum(jnp.dot(normed_local, router_weight, preferred_element_type=jnp....  27.4 us
    gather x5, local copies, waits for them, and re-layouts, route_weights(): picked = jnp.take_along_axis(scores, expert_ids, axis=1)  17 us
    all_gather x1, waiting for transfers between devices, per_device(): gathered = lax.all_gather(hidden_in, 'tp', axis=1, tiled=True)  14.7 us
    reduce_scatter x1, waiting for transfers between devices, per_device(): lax.psum_scatter(shared_part, 'tp', scatter_dimension=1, tiled=True)  14.1 us
    reduce_scatter x1, waiting for transfers between devices, per_device(): reduced = lax.psum_scatter(outputs, 'tp', scatter_dimension=2, tiled=True)  14.1 us
    scatter x1, local copies, waits for them, and re-layouts, slot_table(): slot_weight = jnp.zeros((expert_count * capacity + 1,), jnp.float32).at[t...  8.04 us
  transfers between devices with their start and end apart: 6, of which 5 were waited for; matrix products, arithmetic and copies ran while one was open for 23% of the time, Pallas kernels for 0%

commit v1 on v0

v1 whole, which is shorter than its diff:
```python
import functools

import jax
import jax.numpy as jnp
from jax import lax
from jax.experimental import pallas as pl
from jax.experimental.pallas import tpu as pltpu
from jax.sharding import PartitionSpec as P

CAP = 16
KVR = 512
EPS = 1e-06
ROUTE_SCALE = 2.5
THETA = 10000.0
LANES = 128
F32 = jnp.float32
BF16 = jnp.bfloat16
VMEM = pl.BlockSpec(memory_space=pltpu.VMEM)
SMEM = pl.BlockSpec(memory_space=pltpu.SMEM)


def call(body, out_shape, specs, *operands, flops=1_000_000, limit=None):
    shapes = jax.tree.leaves(out_shape)
    moved = sum(a.size * a.dtype.itemsize for a in operands) + sum(
        s.size * s.dtype.itemsize for s in shapes
    )
    return pl.pallas_call(
        body,
        out_shape=out_shape,
        in_specs=specs,
        out_specs=jax.tree.map(lambda _: VMEM, out_shape),
        cost_estimate=pl.CostEstimate(flops=flops, bytes_accessed=moved, transcendentals=0),
        compiler_params=pltpu.CompilerParams(vmem_limit_bytes=limit),
        name=body.func.__name__ if isinstance(body, functools.partial) else body.__name__,
    )(*operands)


def shape(dims, dtype):
    return jax.ShapeDtypeStruct(dims, dtype)


def dot(a, b):
    return jnp.dot(a, b, preferred_element_type=F32)


def iota(dims, axis):
    return lax.broadcasted_iota(jnp.int32, dims, axis)


def block_at(ref, index, width):
    return pl.ds(pl.multiple_of(index * width, LANES), width)


def transposed_ids(ids):
    rows = ids.shape[0]
    eye = (iota((rows, rows), 0) == iota((rows, rows), 1)).astype(BF16)
    return lax.dot_general(
        ids.astype(F32).astype(BF16), eye, (((0,), (0,)), ((), ())), preferred_element_type=F32
    )


def slot_matrix(ids_t, groups):
    top, rows = ids_t.shape
    expert = iota((groups, rows), 0).astype(F32)
    chosen = jnp.zeros((groups, rows), F32)
    for k in range(top):
        chosen = chosen + jnp.where(ids_t[k : k + 1] == expert, 1.0, 0.0)
    earlier = (iota((rows, rows), 0) < iota((rows, rows), 1)).astype(BF16)
    rank = dot(chosen.astype(BF16), earlier)
    rank = jnp.where(chosen > 0.0, rank, -1.0)
    slot = iota((CAP, rows), 0).astype(F32)
    return jnp.concatenate(
        [jnp.where(rank[e : e + 1] == slot, 1.0, 0.0) for e in range(groups)], axis=0
    )


def pick_rows(groups, ids_ref, hidden_ref, rows_ref):
    chosen = slot_matrix(transposed_ids(ids_ref[...]), groups).astype(BF16)
    rows_ref[...] = dot(chosen, hidden_ref[...]).astype(BF16)


def local_scores(ids_ref, hidden_ref, gain_ref, router_ref, out_ref):
    rows, width = hidden_ref.shape
    member = lax.axis_index("tp")
    x = hidden_ref[...].astype(F32)
    gain = gain_ref[:, block_at(gain_ref, member, width)].astype(F32)
    logits = dot((x * gain).astype(BF16), router_ref[...])
    squares = jnp.sum(x * x, axis=1, keepdims=True)
    both = jnp.concatenate([logits, jnp.broadcast_to(squares, (rows, LANES))], axis=1).T
    experts = router_ref.shape[1]
    ids_t = transposed_ids(ids_ref[...])
    top = ids_t.shape[0]
    index = iota((experts, rows), 0).astype(F32)
    picked = [
        jnp.sum(jnp.where(index == ids_t[k : k + 1], both[:experts], 0.0), axis=0, keepdims=True)
        for k in range(top)
    ]
    out_ref[...] = jnp.concatenate(picked + [both[experts : experts + 8]], axis=0)


def gate_matrix(groups, full_width, ids_ref, mine_ref, theirs_ref, out_ref):
    ids_t = transposed_ids(ids_ref[...])
    top, rows = ids_t.shape
    total = mine_ref[...] + theirs_ref[...]
    inverse = lax.rsqrt(total[top : top + 1] * (1.0 / full_width) + EPS)
    score = 1.0 / (1.0 + jnp.exp(-total[:top] * inverse))
    gate = ROUTE_SCALE * score / jnp.sum(score, axis=0, keepdims=True)
    expert = iota((groups, rows), 0).astype(F32)
    by_expert = jnp.zeros((groups, rows), F32)
    for k in range(top):
        by_expert = by_expert + jnp.where(ids_t[k : k + 1] == expert, gate[k : k + 1], 0.0)
    chosen = slot_matrix(ids_t, groups)
    weights = jnp.concatenate(
        [chosen[e * CAP : (e + 1) * CAP] * by_expert[e : e + 1] for e in range(groups)], axis=0
    ).T
    high = weights.astype(BF16)
    low = (weights - high.astype(F32)).astype(BF16)
    out_ref[...] = jnp.concatenate([high, low], axis=1)


def feed_forward(
    a_ref, b_ref, c_ref, d_ref, gain_ref, gate_ref, up_ref, down_ref, keep_ref, send_ref
):
    width = a_ref.shape[1]
    member = lax.axis_index("tp")
    blocks = [(a_ref, member), (b_ref, member ^ 1), (c_ref, member ^ 2), (d_ref, member ^ 3)]
    squares = 0.0
    for ref, _ in blocks:
        x = ref[...].astype(F32)
        squares = squares + jnp.sum(x * x, axis=1, keepdims=True)
    inverse = lax.rsqrt(squares * (1.0 / (width * len(blocks))) + EPS)
    gate = up = 0.0
    for ref, index in blocks:
        at = block_at(gain_ref, index, width)
        normed = (ref[...].astype(F32) * inverse * gain_ref[:, at].astype(F32)).astype(BF16)
        gate = gate + dot(normed, gate_ref[at, :])
        up = up + dot(normed, up_ref[at, :])
    hidden = (gate / (1.0 + jnp.exp(-gate)) * up).astype(BF16)
    for slot, index in ((0, member ^ 1), (1, member ^ 3)):
        at = block_at(down_ref, index, width)
        send_ref[:, slot * width : (slot + 1) * width] = dot(hidden, down_ref[:, at]).astype(BF16)
    for slot, index in ((0, member), (1, member ^ 2)):
        at = block_at(down_ref, index, width)
        keep_ref[:, slot * width : (slot + 1) * width] = dot(hidden, down_ref[:, at])


def split_pair(value):
    high = value.astype(BF16).astype(F32)
    return high, value - high


def with_energy(latent, energy):
    rows, columns = latent.shape
    padded = -(-(columns + 2) // LANES) * LANES
    lane = iota((rows, padded - columns), 1)
    high, low = split_pair(energy)
    tail = jnp.where(lane == 0, high, jnp.where(lane == 1, low, 0.0))
    return jnp.concatenate([latent, tail], axis=1)


def layer_end(
    pages_ref, routed_ref, gates_ref, hidden_ref, mine_ref, theirs_ref, gain_ref, kv_ref,
    out_ref, keep_ref, send_ref, latent_ref,
):
    member = lax.axis_index("tp")
    rows = routed_ref[...]
    routed = dot(gates_ref[...], jnp.concatenate([rows, rows], axis=0))
    branch = (mine_ref[...] + theirs_ref[...].astype(F32)) + routed
    out = (hidden_ref[...].astype(F32) + branch).astype(BF16)
    out_ref[...] = out
    x = out.astype(F32)
    scaled = (x * gain_ref[...].astype(F32)).astype(BF16)
    energy = jnp.sum(x * x, axis=1, keepdims=True)
    latent_ref[...] = with_energy(dot(scaled, kv_ref[...]), energy)
    page = keep_ref.shape[0] // 2
    for slot, owner in ((0, member), (1, member ^ 2)):
        keep_ref[pl.ds(slot * page, page), :] = latent_ref[page_rows(pages_ref, owner, page), :]
    for slot, owner in ((0, member ^ 1), (1, member ^ 3)):
        send_ref[pl.ds(slot * page, page), :] = latent_ref[
            page_rows(pages_ref, owner, page), :
        ].astype(BF16)


def page_rows(pages_ref, owner, page):
    return pl.ds(pl.multiple_of(pages_ref[0, owner] * page, 16), page)


def latent_half(columns, keep_ref, got_ref, mine_ref, send_ref):
    page = mine_ref.shape[0]
    total = keep_ref[...] + got_ref[...].astype(F32)
    mine_ref[...] = total[:page]
    far = total[page:]
    energy = far[:, columns : columns + 1] + far[:, columns + 1 : columns + 2]
    send_ref[...] = with_energy(far[:, :columns], energy).astype(BF16)


def rope_tables(columns, lengths_ref, pages_ref, cos_ref, sin_ref):
    page = cos_ref.shape[0]
    member = lax.axis_index("tp")
    token = pages_ref[0, member] * page + iota((page, LANES), 0)
    begin = jnp.zeros((page, LANES), jnp.int32)
    start = 0
    for piece in range(lengths_ref.shape[1]):
        begin = jnp.maximum(begin, jnp.where(token >= start, start, 0))
        start = start + lengths_ref[0, piece]
    position = (token - begin).astype(F32)
    half = (columns - KVR) // 2
    lane = iota((page, LANES), 1)
    step = jnp.where(lane < half, lane, lane - half).astype(F32)
    frequency = THETA ** (-step * 2.0 / (2 * half))
    angle = position * frequency
    cos_ref[...] = jnp.cos(angle)
    sine = jnp.sin(angle)
    sin_ref[...] = jnp.where(lane < half, -sine, sine)


def finish(columns, full_width, mine_ref, got_ref, gain_ref, cos_ref, sin_ref, out_ref):
    total = mine_ref[...] + got_ref[...].astype(F32)
    energy = total[:, columns : columns + 1] + total[:, columns + 1 : columns + 2]
    latent = total * lax.rsqrt(energy * (1.0 / full_width) + EPS)
    plain = latent[:, :KVR]
    scale = lax.rsqrt(jnp.mean(plain * plain, axis=1, keepdims=True) + EPS)
    out_ref[:, :KVR] = (plain * scale * gain_ref[...].astype(F32)).astype(BF16)
    rope = latent[:, KVR : KVR + LANES]
    half = (columns - KVR) // 2
    lane = iota(rope.shape, 1)
    other = jnp.where(
        lane < half, pltpu.roll(rope, LANES - half, 1), pltpu.roll(rope, half, 1)
    )
    turned = rope * cos_ref[...] + other * sin_ref[...]
    out_ref[:, KVR:] = turned[:, : columns - KVR].astype(BF16)


def per_device(
    hidden_in,
    moe_gain,
    router_weight,
    expert_ids,
    shared_gate,
    shared_up,
    shared_down,
    expert_gate,
    expert_up,
    expert_down,
    attn_gain,
    kv_down,
    kv_gain,
    doc_lengths,
    page_table,
):
    groups = lax.axis_size("ep")
    members = lax.axis_size("tp")
    rows, width = hidden_in.shape
    full_width = width * members
    slots = groups * CAP
    columns = kv_down.shape[1]
    pages = page_table.shape[1]
    page = rows // pages
    if members != 4 or pages != members or router_weight.shape[1] > 256:
        raise ValueError("unsupported sizes")
    padded = -(-(columns + 2) // LANES) * LANES

    def near(x):
        return lax.ppermute(x, "tp", [(i, i ^ 1) for i in range(members)])

    def far(x):
        return lax.ppermute(x, "tp", [(i, i ^ 2) for i in range(members)])

    def across(x):
        blocks = x.reshape(groups, CAP, width)
        return lax.all_to_all(blocks, "ep", 0, 0, tiled=True).reshape(slots, width)

    gain = moe_gain.reshape(1, full_width)
    far_hidden = far(hidden_in)
    near_hidden = near(hidden_in)
    picked = call(
        functools.partial(pick_rows, groups),
        shape((slots, width), BF16),
        [VMEM] * 2,
        expert_ids,
        hidden_in,
    )
    arrived = across(picked)
    far_rows = far(arrived)
    near_rows = near(arrived)
    diagonal_hidden = near(far_hidden)

    scores = call(
        local_scores,
        shape((16, rows), F32),
        [VMEM] * 4,
        expert_ids,
        hidden_in,
        gain,
        router_weight,
    )
    scores = scores + near(scores)
    far_scores = far(scores)

    def whole_rows(name, a, b, c, d, w_gate, w_up, w_down):
        count = a.shape[0]
        return call(
            feed_forward,
            (shape((count, 2 * width), F32), shape((count, 2 * width), BF16)),
            [VMEM] * 8,
            a,
            b,
            c,
            d,
            gain,
            w_gate,
            w_up,
            w_down,
            flops=6 * count * full_width * w_gate.shape[1],
        )

    def halve(keep, send):
        total = keep + near(send).astype(F32)
        return total[:, :width], total[:, width:].astype(BF16)

    shared_keep, shared_send = whole_rows(
        "shared", hidden_in, near_hidden, far_hidden, diagonal_hidden,
        shared_gate, shared_up, shared_down,
    )
    shared_mine, shared_out = halve(shared_keep, shared_send)
    shared_theirs = far(shared_out)

    diagonal_rows = near(far_rows)
    routed_keep, routed_send = whole_rows(
        "routed", arrived, near_rows, far_rows, diagonal_rows,
        expert_gate[0], expert_up[0], expert_down[0],
    )
    routed_mine, routed_out = halve(routed_keep, routed_send)
    returned = across((routed_mine + far(routed_out).astype(F32)).astype(BF16))

    gates = call(
        functools.partial(gate_matrix, groups, full_width),
        shape((rows, 2 * slots), BF16),
        [VMEM] * 3,
        expert_ids,
        scores,
        far_scores,
    )
    cos, sin = call(
        functools.partial(rope_tables, columns),
        (shape((page, LANES), F32), shape((page, LANES), F32)),
        [SMEM] * 2,
        doc_lengths,
        page_table,
    )
    layer_out, latent_keep, latent_send, _ = call(
        layer_end,
        (
            shape((rows, width), BF16),
            shape((2 * page, padded), F32),
            shape((2 * page, padded), BF16),
            shape((rows, padded), F32),
        ),
        [SMEM] + [VMEM] * 7,
        page_table,
        returned,
        gates,
        hidden_in,
        shared_mine,
        shared_theirs,
        attn_gain.reshape(1, width),
        kv_down,
    )
    latent_mine, latent_out = call(
        functools.partial(latent_half, columns),
        (shape((page, padded), F32), shape((page, padded), BF16)),
        [VMEM] * 2,
        latent_keep,
        near(latent_send),
    )
    page_out = call(
        functools.partial(finish, columns, full_width),
        shape((page, columns), BF16),
        [VMEM] * 5,
        latent_mine,
        far(latent_out),
        kv_gain.reshape(1, KVR),
        cos,
        sin,
    )
    return (layer_out, page_out.reshape(1, 1, page, columns))


def solution(mesh):
    placed = (
        P("ep", "tp"),
        P(),
        P("tp", None),
        P("ep", None),
        P(None, "tp"),
        P(None, "tp"),
        P("tp", None),
        P("ep", None, "tp"),
        P("ep", None, "tp"),
        P("ep", "tp", None),
        P("tp"),
        P("tp", None),
        P(),
        P("ep", None),
        P("ep", None),
    )
    return jax.shard_map(
        per_device,
        mesh=mesh,
        in_specs=placed,
        out_specs=(P("ep", "tp"), P("ep", "tp", None, None)),
        check_vma=False,
    )
```

time: 230 us -> 89.2 us (0.39)
  waiting for transfers between devices: 99.2 us -> 22.5 us
  blocking collectives: 34.9 us -> 0 us
  local copies, waits for them, and re-layouts: 46.6 us -> 12.4 us
  Pallas kernels: 0 us -> 27.6 us
  starting transfers between devices: 5.7 us -> 23.1 us
  matrix products: 14.7 us -> 0 us
  between operations: 14.1 us -> 0.71 us
  other arithmetic: 14.3 us -> 2.3 us
    psum x2 -> x0, waiting for transfers between devices: 55.5 us -> none  [the longest x1 28.2 us: per_device(): latent_sum, energy = lax.psum((latent_part, squares), 'tp')]
    all_to_all x1 -> x0, blocking collectives: 29.1 us -> none  [per_device(): lax.all_to_all(send_rows, 'ep', split_axis=0, concat_axis=0, tiled=True)]
    reduce_scatter x2 -> x0, waiting for transfers between devices: 28.2 us -> none  [the longest x1 14.1 us: per_device(): lax.psum_scatter(shared_part, 'tp', scatter_dimension=1, tiled=True)]
    pallas_call x0 -> x9, Pallas kernels: none -> 27.6 us  [call(): pl.pallas_call(body, out_shape=out_shape, in_specs=specs, out_specs=jax.t...]
    gather x8 -> x0, local copies, waits for them, and re-layouts: 22.3 us -> none  [the longest x5 17 us: route_weights(): picked = jnp.take_along_axis(scores, expert_ids, axis=1)]
    scatter x2 -> x0, local copies, waits for them, and re-layouts: 16.1 us -> none  [the longest x1 8.04 us: slot_table(): slot_weight = jnp.zeros((expert_count * capacity + 1,), jnp.float32).at[t...]
    ppermute x0 -> x14, waiting for transfers between devices: none -> 15.6 us  [the longest x6 11.5 us: far(): return lax.ppermute(x, 'tp', [(i, i ^ 2) for i in range(members)])]
    dot_general x7 -> x0, matrix products: 14.7 us -> none  [the longest x1 6.08 us: per_device(): jnp.dot(shared_hidden, shared_down, preferred_element_type=jnp.float32)]
  transfers between devices with their start and end apart: 6 -> 16, of which waited for: 5 -> 9; matrix products, arithmetic and copies ran while one was open for 23% -> 10% of each run, Pallas kernels for 0% -> 20%
where the time goes in v1:
time: 89.2 us; the launch traced here: 88.6 us
  Pallas kernels  27.6 us (31%)
  starting transfers between devices  23.1 us (26%)
  waiting for transfers between devices  22.5 us (25%)
  local copies, waits for them, and re-layouts  12.4 us (14%)
  other arithmetic  2.3 us (3%)
    pallas_call x9, Pallas kernels, call(): pl.pallas_call(body, out_shape=out_shape, in_specs=specs, out_specs=jax.t...  27.6 us
    all_to_all x2, starting transfers between devices, across(): return lax.all_to_all(blocks, 'ep', 0, 0, tiled=True).reshape(slots, width)  13 us
    ppermute x6, waiting for transfers between devices, far(): return lax.ppermute(x, 'tp', [(i, i ^ 2) for i in range(members)])  11.5 us
    ppermute x6, starting transfers between devices, far(): return lax.ppermute(x, 'tp', [(i, i ^ 2) for i in range(members)])  8.98 us
    unnamed x32, local copies, waits for them, and re-layouts  7.35 us
    all_to_all x2, waiting for transfers between devices, across(): return lax.all_to_all(blocks, 'ep', 0, 0, tiled=True).reshape(slots, width)  6.92 us
    ppermute x8, waiting for transfers between devices, near(): return lax.ppermute(x, 'tp', [(i, i ^ 1) for i in range(members)])  4.04 us
    slice x3, local copies, waits for them, and re-layouts, halve(): return (total[:, :width], total[:, width:].astype(BF16))  1.82 us
  transfers between devices with their start and end apart: 16, of which 9 were waited for; matrix products, arithmetic and copies ran while one was open for 10% of the time, Pallas kernels for 20%

profile of v1, /device:TPU:0, one launch (start us, length us, event | category | flops | bytes accessed | tf_op | source)
XLA Modules:
  0.0 88.6 jit_solution(3280076528258657666)
XLA Ops:
  0.6 1.5 %copy.17.ids_ref = s32[256,8]{1,0:T(8,128)} copy(s32[256,8]{0,1:T(8,128)} %param.18) | data formatting | bytes 16384 | tf_op args[3]
  2.1 2.3 %pick_rows.1 = bf16[128,896]{1,0:T(8,128)(2,1)} custom-call(s32[256,8]{1,0:T(8,128)} %copy.17.ids_ref, bf16[256,896]{1,0:T(8,128)(2,1)} %hidden_ref.5), custom_call_target="tpu_custom_call" | custom-call | flops 1000000 | bytes 696320 | tf_op jit(solution)/shard_map/pick_rows/pallas_call | solution.py:27
  4.4 7.3 %all-to-all-start = ((bf16[8,16,896]{2,1,0:T(8,128)(2,1)}), bf16[8,16,896]{2,1,0:T(8,128)(2,1)S(1)}, u32[]{:S(2)}, u32[]{:S(2)}) async-start(bf16[8,16,896]{2,1,0:T(8,128)(2,1)} %bitcast.12), calls=%async_computation | async-start | bytes 458752 | tf_op jit(solution)/shard_map/all_to_all | solution.py:271
  11.7 1.5 %collective-permute-start.8 = (bf16[256,896]{1,0:T(8,128)(2,1)}, bf16[256,896]{1,0:T(8,128)(2,1)S(1)}, u32[]{:S(2)}, u32[]{:S(2)}) collective-permute-start(bf16[256,896]{1,0:T(8,128)(2,1)} %hidden_ref.5), channel_id=1, source_target_pairs={{0,2},{1,3},{2,0},{3,1},{4,6},{5,7},{6,4},{7,5},{8,10},{9,11},{10,... | collective-permute-start | bytes 1376264 | tf_op jit(solution)/shard_map/ppermute | solution.py:267
  13.2 6.9 %all-to-all-done = bf16[8,16,896]{2,1,0:T(8,128)(2,1)S(1)} async-done(((bf16[8,16,896]{2,1,0:T(8,128)(2,1)}), bf16[8,16,896]{2,1,0:T(8,128)(2,1)S(1)}, u32[]{:S(2)}, u32[]{:S(2)}) %all-to-all-start) | async-done | bytes 229408 | tf_op jit(solution)/shard_map/all_to_all | solution.py:271
  20.1 1.5 %collective-permute-start.1 = (bf16[128,896]{1,0:T(8,128)(2,1)S(1)}, bf16[128,896]{1,0:T(8,128)(2,1)S(1)}, u32[]{:S(2)}, u32[]{:S(2)}) collective-permute-start(bf16[128,896]{1,0:T(8,128)(2,1)S(1)} %bitcast.13), channel_id=1, source_target_pairs={{0,2},{1,3},{2,0},{3,1},{4,6},{5,7},{6,4},{7,5},{8,10},{9,11},{10,... | collective-permute-start | bytes 688136 | tf_op jit(solution)/shard_map/ppermute | solution.py:267
  21.6 0.0 collective-permute-start.7
  21.6 3.6 %collective-permute-done.8.c_ref = bf16[256,896]{1,0:T(8,128)(2,1)S(1)} collective-permute-done((bf16[256,896]{1,0:T(8,128)(2,1)}, bf16[256,896]{1,0:T(8,128)(2,1)S(1)}, u32[]{:S(2)}, u32[]{:S(2)}) %collective-permute-start.8) | collective-permute-done | bytes 458784 | tf_op jit(solution)/shard_map/ppermute | solution.py:267
  25.3 0.0 collective-permute-start.9
  25.3 0.5 collective-permute-start
  25.8 3.0 %collective-permute-done.1.c_ref = bf16[128,896]{1,0:T(8,128)(2,1)S(1)} collective-permute-done((bf16[128,896]{1,0:T(8,128)(2,1)S(1)}, bf16[128,896]{1,0:T(8,128)(2,1)S(1)}, u32[]{:S(2)}, u32[]{:S(2)}) %collective-permute-start.1) | collective-permute-done | bytes 229408 | tf_op jit(solution)/shard_map/ppermute | solution.py:267
  28.8 0.0 collective-permute-start.2
  28.8 1.3 %reshape.30.gain_ref = bf16[1,3584]{1,0:T(2,128)(2,1)} reshape(bf16[3584]{0:T(1024)(128)(2,1)} %param.16) | data formatting | bytes 14336 | tf_op jit(solution)/shard_map/reshape | solution.py:273
  30.1 0.0 collective-permute-done.b_ref
  30.1 0.2 collective-permute-done.2.d_ref
  30.3 0.0 copy-done.9
  30.3 0.5 copy-done.10
  30.8 0.2 copy-done.11
  31.0 5.3 %feed_forward.2 = (f32[128,1792]{1,0:T(8,128)}, bf16[128,1792]{1,0:T(8,128)(2,1)}) custom-call(bf16[128,896]{1,0:T(8,128)(2,1)} %bitcast.15, bf16[128,896]{1,0:T(8,128)(2,1)} %copy-done.10, bf16[128,896]{1,0:T(8,128)(2,1)} %copy-done.9, bf16[128,896]{1,0:T(8,128)(2,1)} %copy-done.11, bf16[1,3584]{1,0:T(2,128)(2,1)} %reshape.30.gain_ref, ...), custom_call_target="tpu_custom_call" | custom-call | flops 704643072 | bytes 7805952 | tf_op jit(solution)/shard_map/feed_forward/pallas_call | solution.py:27
  36.3 0.0 copy-done.6
  36.3 0.5 collective-permute-start.3
  36.7 0.0 collective-permute-done.7.b_ref
  36.8 0.0 collective-permute-done.9.d_ref
  36.8 0.8 copy-done.7
  37.5 0.8 copy-done.8
  38.3 6.7 %feed_forward.3 = (f32[256,1792]{1,0:T(8,128)}, bf16[256,1792]{1,0:T(8,128)(2,1)}) custom-call(bf16[256,896]{1,0:T(8,128)(2,1)} %hidden_ref.5, bf16[256,896]{1,0:T(8,128)(2,1)} %copy-done.7, bf16[256,896]{1,0:T(8,128)(2,1)} %copy-done.6, bf16[256,896]{1,0:T(8,128)(2,1)} %copy-done.8, bf16[1,3584]{1,0:T(2,128)(2,1)} %reshape.30.gain_ref, ...), custom_call_target="tpu_custom_call" | custom-call | flops 1409286144 | bytes 10099712 | tf_op jit(solution)/shard_map/feed_forward/pallas_call | solution.py:27
  45.0 0.1 collective-permute-start.10
  45.1 0.0 collective-permute-done.3
  45.1 0.1 convert_add_fusion.1
  45.3 1.6 %collective-permute-start.4 = (bf16[128,896]{1,0:T(8,128)(2,1)S(1)}, bf16[128,896]{1,0:T(8,128)(2,1)S(1)}, u32[]{:S(2)}, u32[]{:S(2)}) collective-permute-start(bf16[128,896]{1,0:T(8,128)(2,1)S(1)} %slice.28), channel_id=1, source_target_pairs={{0,2},{1,3},{2,0},{3,1},{4,6},{5,7},{6,4},{7,5},{8,10},{9,11},{10,... | collective-permute-start | bytes 688136 | tf_op jit(solution)/shard_map/ppermute | solution.py:267
  46.8 0.9 %collective-permute-done.10 = bf16[256,1792]{1,0:T(8,128)(2,1)S(1)} collective-permute-done((bf16[256,1792]{1,0:T(8,128)(2,1)}, bf16[256,1792]{1,0:T(8,128)(2,1)S(1)}, u32[]{:S(2)}, u32[]{:S(2)}) %collective-permute-start.10) | collective-permute-done | bytes 917536 | tf_op jit(solution)/shard_map/ppermute | solution.py:264
  47.7 0.0 copy-done
  47.7 0.2 convert_add_fusion
  47.9 0.0 copy-start.1
  47.9 0.8 slice.27
  48.7 1.5 %collective-permute-start.11 = (bf16[256,896]{1,0:T(8,128)(2,1)}, bf16[256,896]{1,0:T(8,128)(2,1)S(1)}, u32[]{:S(2)}, u32[]{:S(2)}) collective-permute-start(bf16[256,896]{1,0:T(8,128)(2,1)} %slice.27), channel_id=1, source_target_pairs={{0,2},{1,3},{2,0},{3,1},{4,6},{5,7},{6,4},{7,5},{8,10},{9,11},{10,... | collective-permute-start | bytes 1376264 | tf_op jit(solution)/shard_map/ppermute | solution.py:267
  50.2 3.6 %collective-permute-done.4 = bf16[128,896]{1,0:T(8,128)(2,1)S(1)} collective-permute-done((bf16[128,896]{1,0:T(8,128)(2,1)S(1)}, bf16[128,896]{1,0:T(8,128)(2,1)S(1)}, u32[]{:S(2)}, u32[]{:S(2)}) %collective-permute-start.4) | collective-permute-done | bytes 229408 | tf_op jit(solution)/shard_map/ppermute | solution.py:267
  53.8 0.7 fusion
  54.5 5.7 %all-to-all-start.1 = ((bf16[8,16,896]{2,1,0:T(8,128)(2,1)}), bf16[8,16,896]{2,1,0:T(8,128)(2,1)S(1)}, u32[]{:S(2)}, u32[]{:S(2)}) async-start(bf16[8,16,896]{2,1,0:T(8,128)(2,1)} %bitcast.5), calls=%async_computation.1 | async-start | bytes 458752 | tf_op jit(solution)/shard_map/all_to_all | solution.py:271
  60.2 2.4 %local_scores.1 = f32[16,256]{1,0:T(8,128)} custom-call(s32[256,8]{1,0:T(8,128)} %copy.17.ids_ref, bf16[256,896]{1,0:T(8,128)(2,1)} %hidden_ref.5, bf16[1,3584]{1,0:T(2,128)(2,1)} %reshape.30.gain_ref, bf16[896,256]{1,0:T(8,128)(2,1)} %router_ref.1), custom_call_target="tpu_custom_call" | custom-call | flops 1000000 | bytes 949248 | tf_op jit(solution)/shard_map/local_scores/pallas_call | solution.py:27
  62.6 0.0 collective-permute-start.5
  62.6 1.4 %collective-permute-done.5 = f32[16,256]{1,0:T(8,128)S(1)} collective-permute-done((f32[16,256]{1,0:T(8,128)}, f32[16,256]{1,0:T(8,128)S(1)}, u32[]{:S(2)}, u32[]{:S(2)}) %collective-permute-start.5) | collective-permute-done | bytes 16416 | tf_op jit(solution)/shard_map/ppermute | solution.py:264
  64.0 1.3 %add.14.mine_ref = f32[16,256]{1,0:T(8,128)} add(f32[16,256]{1,0:T(8,128)} %local_scores.1, f32[16,256]{1,0:T(8,128)S(1)} %collective-permute-done.5) | non-fusion elementwise | flops 4096 | bytes 49152 | tf_op jit(solution)/shard_map/add | solution.py:297
  65.3 1.5 %collective-permute-start.6 = (f32[16,256]{1,0:T(8,128)}, f32[16,256]{1,0:T(8,128)}, u32[]{:S(2)}, u32[]{:S(2)}) collective-permute-start(f32[16,256]{1,0:T(8,128)} %add.14.mine_ref), channel_id=1, source_target_pairs={{0,2},{1,3},{2,0},{3,1},{4,6},{5,7},{6,4},{7,5},{8,10},{9,11},{10,... | collective-permute-start | bytes 49160 | tf_op jit(solution)/shard_map/ppermute | solution.py:267
  66.9 1.5 %copy.20.kv_ref = bf16[896,576]{1,0:T(8,128)(2,1)} copy(bf16[896,576]{0,1:T(8,128)(2,1)S(1)} %copy-done.1) | data formatting | bytes 2064384 | tf_op args[11]
  68.3 1.3 %reshape.33.gain_ref = bf16[1,896]{1,0:T(2,128)(2,1)} reshape(bf16[896]{0:T(1024)(128)(2,1)} %param.25) | data formatting | bytes 3584 | tf_op jit(solution)/shard_map/reshape | solution.py:366
  69.6 0.0 collective-permute-done.6.theirs_ref
  69.6 2.0 %gate_matrix.1.gates_ref = bf16[256,256]{1,0:T(8,128)(2,1)} custom-call(s32[256,8]{1,0:T(8,128)} %copy.17.ids_ref, f32[16,256]{1,0:T(8,128)} %add.14.mine_ref, f32[16,256]{1,0:T(8,128)} %collective-permute-done.6.theirs_ref), custom_call_target="tpu_custom_call" | custom-call | flops 1000000 | bytes 172032 | tf_op jit(solution)/shard_map/gate_matrix/pallas_call | solution.py:27
  71.6 1.0 %slice.20.mine_ref = f32[256,896]{1,0:T(8,128)} slice(f32[256,1792]{1,0:T(8,128)S(1)} %convert_add_fusion), slice={[0:256], [0:896]} | slice | bytes 1835008 | tf_op jit(solution)/shard_map/slice | solution.py:319
  72.6 0.0 all-to-all-done.1
  72.6 0.0 collective-permute-done.11.theirs_ref
  72.6 0.7 copy-done.2
  73.3 0.2 copy-done.5
  73.4 3.7 %layer_end.1 = (bf16[256,896]{1,0:T(8,128)(2,1)}, f32[128,640]{1,0:T(8,128)}, bf16[128,640]{1,0:T(8,128)(2,1)}, f32[256,640]{1,0:T(8,128)}) custom-call(s32[1,4]{1,0:T(1,128)} %pages_ref.3, bf16[128,896]{1,0:T(8,128)(2,1)} %bitcast.11, bf16[256,256]{1,0:T(8,128)(2,1)} %gate_matrix.1.gates_ref, bf16[256,896]{1,0:T(8,128)(2,1)} %hidden_ref.5, ...), custom_call_target="tpu_custom_call" | custom-call | flops 1000000 | bytes 4835088 | tf_op jit(solution)/shard_map/layer_end/pallas_call | solution.py:27
  77.2 0.0 collective-permute-start.12
  77.2 1.6 %collective-permute-done.12.got_ref = bf16[128,640]{1,0:T(8,128)(2,1)S(1)} collective-permute-done((bf16[128,640]{1,0:T(8,128)(2,1)}, bf16[128,640]{1,0:T(8,128)(2,1)S(1)}, u32[]{:S(2)}, u32[]{:S(2)}) %collective-permute-start.12) | collective-permute-done | bytes 163872 | tf_op jit(solution)/shard_map/ppermute | solution.py:264
  78.8 0.7 copy-done.12
  79.4 1.9 %latent_half.1 = (f32[64,640]{1,0:T(8,128)}, bf16[64,640]{1,0:T(8,128)(2,1)}) custom-call(f32[128,640]{1,0:T(8,128)} %get-tuple-element.18.keep_ref, bf16[128,640]{1,0:T(8,128)(2,1)} %copy-done.12), custom_call_target="tpu_custom_call" | custom-call | flops 1000000 | bytes 737280 | tf_op jit(solution)/shard_map/latent_half/pallas_call | solution.py:27
  81.3 1.3 %collective-permute-start.13 = (bf16[64,640]{1,0:T(8,128)(2,1)}, bf16[64,640]{1,0:T(8,128)(2,1)S(1)}, u32[]{:S(2)}, u32[]{:S(2)}) collective-permute-start(bf16[64,640]{1,0:T(8,128)(2,1)} %get-tuple-element.21), channel_id=1, source_target_pairs={{0,2},{1,3},{2,0},{3,1},{4,6},{5,7},{6,4},{7,5},{8,10},{9,11},{10,... | collective-permute-start | bytes 245768 | tf_op jit(solution)/shard_map/ppermute | solution.py:267
  82.6 0.6 reshape.34.gain_ref
  83.2 1.5 %rope_tables.1 = (f32[64,128]{1,0:T(8,128)}, f32[64,128]{1,0:T(8,128)}) custom-call(s32[1,4]{1,0:T(1,128)} %lengths_ref.1, s32[1,4]{1,0:T(1,128)} %pages_ref.3), custom_call_target="tpu_custom_call" | custom-call | flops 1000000 | bytes 65568 | tf_op jit(solution)/shard_map/rope_tables/pallas_call | solution.py:27
  84.7 1.3 %collective-permute-done.13.got_ref = bf16[64,640]{1,0:T(8,128)(2,1)S(1)} collective-permute-done((bf16[64,640]{1,0:T(8,128)(2,1)}, bf16[64,640]{1,0:T(8,128)(2,1)S(1)}, u32[]{:S(2)}, u32[]{:S(2)}) %collective-permute-start.13) | collective-permute-done | bytes 81952 | tf_op jit(solution)/shard_map/ppermute | solution.py:267
  86.0 0.6 copy-done.13
  86.7 1.9 %finish.1 = bf16[64,576]{1,0:T(8,128)(2,1)} custom-call(f32[64,640]{1,0:T(8,128)} %get-tuple-element.20.mine_ref, bf16[64,640]{1,0:T(8,128)(2,1)} %copy-done.13, bf16[1,512]{1,0:T(2,128)(2,1)} %reshape.34.gain_ref, f32[64,128]{1,0:T(8,128)} %get-tuple-element.22.cos_ref, f32[64,128]{1,0:T(8,128)} %get-tuple-element.23.sin_ref), custom_call_target="tpu_custom_call" | custom-call | flops 1000000 | bytes 386048 | tf_op jit(solution)/shard_map/finish/pallas_call | solution.py:27
  (19 shorter events, 0.1 us)
Async XLA Ops:
  4.4 15.7 %all-to-all-start = ((bf16[8,16,896]{2,1,0:T(8,128)(2,1)}), bf16[8,16,896]{2,1,0:T(8,128)(2,1)S(1)}, u32[]{:S(2)}, u32[]{:S(2)}) async-start(bf16[8,16,896]{2,1,0:T(8,128)(2,1)} %bitcast.12), calls=%async_computation | async-start | bytes 458752 | tf_op jit(solution)/shard_map/all_to_all | solution.py:271
  11.7 13.6 %collective-permute-start.8 = (bf16[256,896]{1,0:T(8,128)(2,1)}, bf16[256,896]{1,0:T(8,128)(2,1)S(1)}, u32[]{:S(2)}, u32[]{:S(2)}) collective-permute-start(bf16[256,896]{1,0:T(8,128)(2,1)} %hidden_ref.5), channel_id=1, source_target_pairs={{0,2},{1,3},{2,0},{3,1},{4,6},{5,7},{6,4},{7,5},{8,10},{9,11},{10,... | collective-permute-start | bytes 1376264 | tf_op jit(solution)/shard_map/ppermute | solution.py:267
  20.1 10.2 %copy-start.4 = (bf16[8,16,896]{2,1,0:T(8,128)(2,1)}, bf16[8,16,896]{2,1,0:T(8,128)(2,1)S(1)}, u32[]{:S(2)}) copy-start(bf16[8,16,896]{2,1,0:T(8,128)(2,1)S(1)} %all-to-all-done) | copy-start | bytes 688132
  20.1 8.7 %collective-permute-start.1 = (bf16[128,896]{1,0:T(8,128)(2,1)S(1)}, bf16[128,896]{1,0:T(8,128)(2,1)S(1)}, u32[]{:S(2)}, u32[]{:S(2)}) collective-permute-start(bf16[128,896]{1,0:T(8,128)(2,1)S(1)} %bitcast.13), channel_id=1, source_target_pairs={{0,2},{1,3},{2,0},{3,1},{4,6},{5,7},{6,4},{7,5},{8,10},{9,11},{10,... | collective-permute-start | bytes 688136 | tf_op jit(solution)/shard_map/ppermute | solution.py:267
  21.6 15.1 %collective-permute-start.7 = (bf16[256,896]{1,0:T(8,128)(2,1)}, bf16[256,896]{1,0:T(8,128)(2,1)S(1)}, u32[]{:S(2)}, u32[]{:S(2)}) collective-permute-start(bf16[256,896]{1,0:T(8,128)(2,1)} %hidden_ref.5), channel_id=1, source_target_pairs={{0,1},{1,0},{2,3},{3,2},{4,5},{5,4},{6,7},{7,6},{8,9},{9,8},{10,11... | collective-permute-start | bytes 1376264 | tf_op jit(solution)/shard_map/ppermute | solution.py:264
  25.3 11.0 %copy-start.6 = (bf16[256,896]{1,0:T(8,128)(2,1)}, bf16[256,896]{1,0:T(8,128)(2,1)S(1)}, u32[]{:S(2)}) copy-start(bf16[256,896]{1,0:T(8,128)(2,1)S(1)} %collective-permute-done.8.c_ref) | copy-start | bytes 1376260
  25.3 11.5 %collective-permute-start.9 = (bf16[256,896]{1,0:T(8,128)(2,1)S(1)}, bf16[256,896]{1,0:T(8,128)(2,1)S(1)}, u32[]{:S(2)}, u32[]{:S(2)}) collective-permute-start(bf16[256,896]{1,0:T(8,128)(2,1)S(1)} %collective-permute-done.8.c_ref), channel_id=1, source_target_pairs={{0,1},{1,0},{2,3},{3,2},{4,5},{5,4},{6,7},{7,6},{8,9},{9,8},{10,11... | collective-permute-start | bytes 1376264 | tf_op jit(solution)/shard_map/ppermute | solution.py:264
  25.3 4.8 %collective-permute-start = (bf16[128,896]{1,0:T(8,128)(2,1)S(1)}, bf16[128,896]{1,0:T(8,128)(2,1)S(1)}, u32[]{:S(2)}, u32[]{:S(2)}) collective-permute-start(bf16[128,896]{1,0:T(8,128)(2,1)S(1)} %bitcast.14), channel_id=1, source_target_pairs={{0,1},{1,0},{2,3},{3,2},{4,5},{5,4},{6,7},{7,6},{8,9},{9,8},{10,11... | collective-permute-start | bytes 688136 | tf_op jit(solution)/shard_map/ppermute | solution.py:264
  28.8 1.5 %copy-start.9 = (bf16[128,896]{1,0:T(8,128)(2,1)}, bf16[128,896]{1,0:T(8,128)(2,1)S(1)}, u32[]{:S(2)}) copy-start(bf16[128,896]{1,0:T(8,128)(2,1)S(1)} %collective-permute-done.1.c_ref) | copy-start | bytes 688132
  28.8 1.5 %collective-permute-start.2 = (bf16[128,896]{1,0:T(8,128)(2,1)S(1)}, bf16[128,896]{1,0:T(8,128)(2,1)S(1)}, u32[]{:S(2)}, u32[]{:S(2)}) collective-permute-start(bf16[128,896]{1,0:T(8,128)(2,1)S(1)} %collective-permute-done.1.c_ref), channel_id=1, source_target_pairs={{0,1},{1,0},{2,3},{3,2},{4,5},{5,4},{6,7},{7,6},{8,9},{9,8},{10,11... | collective-permute-start | bytes 688136 | tf_op jit(solution)/shard_map/ppermute | solution.py:264
  30.1 0.7 copy-start.10
  30.3 0.7 copy-start.11
  36.3 8.9 %copy-start.3 = (f32[128,1792]{1,0:T(8,128)S(1)}, f32[128,1792]{1,0:T(8,128)}, u32[]{:S(2)}) copy-start(f32[128,1792]{1,0:T(8,128)} %get-tuple-element.13) | copy-start | bytes 2752516
  36.3 8.9 %collective-permute-start.3 = (bf16[128,1792]{1,0:T(8,128)(2,1)}, bf16[128,1792]{1,0:T(8,128)(2,1)S(1)}, u32[]{:S(2)}, u32[]{:S(2)}) collective-permute-start(bf16[128,1792]{1,0:T(8,128)(2,1)} %get-tuple-element.14), channel_id=1, source_target_pairs={{0,1},{1,0},{2,3},{3,2},{4,5},{5,4},{6,7},{7,6},{8,9},{9,8},{10,11... | collective-permute-start | bytes 1376264 | tf_op jit(solution)/shard_map/ppermute | solution.py:264
  36.7 0.8 copy-start.7
  37.5 0.8 copy-start.8
  45.0 2.7 %copy-start = (f32[256,1792]{1,0:T(8,128)S(1)}, f32[256,1792]{1,0:T(8,128)}, u32[]{:S(2)}) copy-start(f32[256,1792]{1,0:T(8,128)} %get-tuple-element.15) | copy-start | bytes 5505028
  45.0 2.7 %collective-permute-start.10 = (bf16[256,1792]{1,0:T(8,128)(2,1)}, bf16[256,1792]{1,0:T(8,128)(2,1)S(1)}, u32[]{:S(2)}, u32[]{:S(2)}) collective-permute-start(bf16[256,1792]{1,0:T(8,128)(2,1)} %get-tuple-element.16), channel_id=1, source_target_pairs={{0,1},{1,0},{2,3},{3,2},{4,5},{5,4},{6,7},{7,6},{8,9},{9,8},{10,11... | collective-permute-start | bytes 2752520 | tf_op jit(solution)/shard_map/ppermute | solution.py:264
  45.3 8.5 %collective-permute-start.4 = (bf16[128,896]{1,0:T(8,128)(2,1)S(1)}, bf16[128,896]{1,0:T(8,128)(2,1)S(1)}, u32[]{:S(2)}, u32[]{:S(2)}) collective-permute-start(bf16[128,896]{1,0:T(8,128)(2,1)S(1)} %slice.28), channel_id=1, source_target_pairs={{0,2},{1,3},{2,0},{3,1},{4,6},{5,7},{6,4},{7,5},{8,10},{9,11},{10,... | collective-permute-start | bytes 688136 | tf_op jit(solution)/shard_map/ppermute | solution.py:267
  47.9 19.0 %copy-start.1 = (bf16[896,576]{0,1:T(8,128)(2,1)S(1)}, bf16[896,576]{0,1:T(8,128)(2,1)}, u32[]{:S(2)}) copy-start(bf16[896,576]{0,1:T(8,128)(2,1)} %param.26) | copy-start | bytes 3096580
  48.7 23.9 %collective-permute-start.11 = (bf16[256,896]{1,0:T(8,128)(2,1)}, bf16[256,896]{1,0:T(8,128)(2,1)S(1)}, u32[]{:S(2)}, u32[]{:S(2)}) collective-permute-start(bf16[256,896]{1,0:T(8,128)(2,1)} %slice.27), channel_id=1, source_target_pairs={{0,2},{1,3},{2,0},{3,1},{4,6},{5,7},{6,4},{7,5},{8,10},{9,11},{10,... | collective-permute-start | bytes 1376264 | tf_op jit(solution)/shard_map/ppermute | solution.py:267
  54.5 18.0 %all-to-all-start.1 = ((bf16[8,16,896]{2,1,0:T(8,128)(2,1)}), bf16[8,16,896]{2,1,0:T(8,128)(2,1)S(1)}, u32[]{:S(2)}, u32[]{:S(2)}) async-start(bf16[8,16,896]{2,1,0:T(8,128)(2,1)} %bitcast.5), calls=%async_computation.1 | async-start | bytes 458752 | tf_op jit(solution)/shard_map/all_to_all | solution.py:271
  62.6 1.4 %collective-permute-start.5 = (f32[16,256]{1,0:T(8,128)}, f32[16,256]{1,0:T(8,128)S(1)}, u32[]{:S(2)}, u32[]{:S(2)}) collective-permute-start(f32[16,256]{1,0:T(8,128)} %local_scores.1), channel_id=1, source_target_pairs={{0,1},{1,0},{2,3},{3,2},{4,5},{5,4},{6,7},{7,6},{8,9},{9,8},{10,11... | collective-permute-start | bytes 49160 | tf_op jit(solution)/shard_map/ppermute | solution.py:264
  65.3 4.3 %collective-permute-start.6 = (f32[16,256]{1,0:T(8,128)}, f32[16,256]{1,0:T(8,128)}, u32[]{:S(2)}, u32[]{:S(2)}) collective-permute-start(f32[16,256]{1,0:T(8,128)} %add.14.mine_ref), channel_id=1, source_target_pairs={{0,2},{1,3},{2,0},{3,1},{4,6},{5,7},{6,4},{7,5},{8,10},{9,11},{10,... | collective-permute-start | bytes 49160 | tf_op jit(solution)/shard_map/ppermute | solution.py:267
  72.6 0.7 copy-start.2
  72.6 0.8 copy-start.5
  73.4 9.2 %copy-start.14 = (bf16[512]{0:T(512)(128)(2,1)S(1)}, bf16[512]{0:T(512)(128)(2,1)}, u32[]{:S(2)}) copy-start(bf16[512]{0:T(512)(128)(2,1)} %param.27) | copy-start | bytes 3076
  77.2 1.6 %collective-permute-start.12 = (bf16[128,640]{1,0:T(8,128)(2,1)}, bf16[128,640]{1,0:T(8,128)(2,1)S(1)}, u32[]{:S(2)}, u32[]{:S(2)}) collective-permute-start(bf16[128,640]{1,0:T(8,128)(2,1)} %get-tuple-element.19), channel_id=1, source_target_pairs={{0,1},{1,0},{2,3},{3,2},{4,5},{5,4},{6,7},{7,6},{8,9},{9,8},{10,11... | collective-permute-start | bytes 491528 | tf_op jit(solution)/shard_map/ppermute | solution.py:264
  78.8 0.7 copy-start.12
  81.3 4.7 %collective-permute-start.13 = (bf16[64,640]{1,0:T(8,128)(2,1)}, bf16[64,640]{1,0:T(8,128)(2,1)S(1)}, u32[]{:S(2)}, u32[]{:S(2)}) collective-permute-start(bf16[64,640]{1,0:T(8,128)(2,1)} %get-tuple-element.21), channel_id=1, source_target_pairs={{0,2},{1,3},{2,0},{3,1},{4,6},{5,7},{6,4},{7,5},{8,10},{9,11},{10,... | collective-permute-start | bytes 245768 | tf_op jit(solution)/shard_map/ppermute | solution.py:267
  86.0 0.6 copy-start.13

commit v2 on v1

--- a/solution.py
+++ b/solution.py
@@ -19,19 +19,20 @@
 SMEM = pl.BlockSpec(memory_space=pltpu.SMEM)
 
 
-def call(body, out_shape, specs, *operands, flops=1_000_000, limit=None):
+def call(body, out_shape, specs, *operands, flops=1_000_000, scratch=()):
     shapes = jax.tree.leaves(out_shape)
     moved = sum(a.size * a.dtype.itemsize for a in operands) + sum(
         s.size * s.dtype.itemsize for s in shapes
     )
+    limit = min(2 * moved + (4 << 20), 60 << 20)
     return pl.pallas_call(
         body,
         out_shape=out_shape,
         in_specs=specs,
         out_specs=jax.tree.map(lambda _: VMEM, out_shape),
+        scratch_shapes=scratch,
         cost_estimate=pl.CostEstimate(flops=flops, bytes_accessed=moved, transcendentals=0),
         compiler_params=pltpu.CompilerParams(vmem_limit_bytes=limit),
-        name=body.func.__name__ if isinstance(body, functools.partial) else body.__name__,
     )(*operands)
 
 
@@ -43,20 +44,16 @@
     return jnp.dot(a, b, preferred_element_type=F32)
 
 
+def dot_t(a, b):
+    return lax.dot_general(a, b, (((1,), (1,)), ((), ())), preferred_element_type=F32)
+
+
 def iota(dims, axis):
     return lax.broadcasted_iota(jnp.int32, dims, axis)
 
 
-def block_at(ref, index, width):
+def block_at(index, width):
     return pl.ds(pl.multiple_of(index * width, LANES), width)
-
-
-def transposed_ids(ids):
-    rows = ids.shape[0]
-    eye = (iota((rows, rows), 0) == iota((rows, rows), 1)).astype(BF16)
-    return lax.dot_general(
-        ids.astype(F32).astype(BF16), eye, (((0,), (0,)), ((), ())), preferred_element_type=F32
-    )
 
 
 def slot_matrix(ids_t, groups):
@@ -75,7 +72,7 @@
 
 
 def pick_rows(groups, ids_ref, hidden_ref, rows_ref):
-    chosen = slot_matrix(transposed_ids(ids_ref[...]), groups).astype(BF16)
+    chosen = slot_matrix(ids_ref[...].astype(F32), groups).astype(BF16)
     rows_ref[...] = dot(chosen, hidden_ref[...]).astype(BF16)
 
 
@@ -83,12 +80,12 @@
     rows, width = hidden_ref.shape
     member = lax.axis_index("tp")
     x = hidden_ref[...].astype(F32)
-    gain = gain_ref[:, block_at(gain_ref, member, width)].astype(F32)
+    gain = gain_ref[:, block_at(member, width)].astype(F32)
     logits = dot((x * gain).astype(BF16), router_ref[...])
     squares = jnp.sum(x * x, axis=1, keepdims=True)
     both = jnp.concatenate([logits, jnp.broadcast_to(squares, (rows, LANES))], axis=1).T
     experts = router_ref.shape[1]
-    ids_t = transposed_ids(ids_ref[...])
+    ids_t = ids_ref[...].astype(F32)
     top = ids_t.shape[0]
     index = iota((experts, rows), 0).astype(F32)
     picked = [
@@ -99,7 +96,7 @@
 
 
 def gate_matrix(groups, full_width, ids_ref, mine_ref, theirs_ref, out_ref):
-    ids_t = transposed_ids(ids_ref[...])
+    ids_t = ids_ref[...].astype(F32)
     top, rows = ids_t.shape
     total = mine_ref[...] + theirs_ref[...]
     inverse = lax.rsqrt(total[top : top + 1] * (1.0 / full_width) + EPS)
@@ -119,7 +116,8 @@
 
 
 def feed_forward(
-    a_ref, b_ref, c_ref, d_ref, gain_ref, gate_ref, up_ref, down_ref, keep_ref, send_ref
+    a_ref, b_ref, c_ref, d_ref, gain_ref, gate_ref, up_ref, down_ref,
+    mine_ref, far_ref, send_ref,
 ):
     width = a_ref.shape[1]
     member = lax.axis_index("tp")
@@ -131,17 +129,16 @@
     inverse = lax.rsqrt(squares * (1.0 / (width * len(blocks))) + EPS)
     gate = up = 0.0
     for ref, index in blocks:
-        at = block_at(gain_ref, index, width)
+        at = block_at(index, width)
         normed = (ref[...].astype(F32) * inverse * gain_ref[:, at].astype(F32)).astype(BF16)
         gate = gate + dot(normed, gate_ref[at, :])
         up = up + dot(normed, up_ref[at, :])
     hidden = (gate / (1.0 + jnp.exp(-gate)) * up).astype(BF16)
     for slot, index in ((0, member ^ 1), (1, member ^ 3)):
-        at = block_at(down_ref, index, width)
+        at = block_at(index, width)
         send_ref[:, slot * width : (slot + 1) * width] = dot(hidden, down_ref[:, at]).astype(BF16)
-    for slot, index in ((0, member), (1, member ^ 2)):
-        at = block_at(down_ref, index, width)
-        keep_ref[:, slot * width : (slot + 1) * width] = dot(hidden, down_ref[:, at])
+    for ref, index in ((far_ref, member ^ 2), (mine_ref, member)):
+        ref[...] = dot(hidden, down_ref[:, block_at(index, width)])
 
 
 def split_pair(value):
@@ -159,19 +156,18 @@
 
 
 def layer_end(
-    pages_ref, routed_ref, gates_ref, hidden_ref, mine_ref, theirs_ref, gain_ref, kv_ref,
+    pages_ref, routed_ref, gates_ref, base_ref, gain_ref, kv_ref,
     out_ref, keep_ref, send_ref, latent_ref,
 ):
     member = lax.axis_index("tp")
     rows = routed_ref[...]
     routed = dot(gates_ref[...], jnp.concatenate([rows, rows], axis=0))
-    branch = (mine_ref[...] + theirs_ref[...].astype(F32)) + routed
-    out = (hidden_ref[...].astype(F32) + branch).astype(BF16)
+    out = (base_ref[...] + routed).astype(BF16)
     out_ref[...] = out
     x = out.astype(F32)
     scaled = (x * gain_ref[...].astype(F32)).astype(BF16)
     energy = jnp.sum(x * x, axis=1, keepdims=True)
-    latent_ref[...] = with_energy(dot(scaled, kv_ref[...]), energy)
+    latent_ref[...] = with_energy(dot_t(scaled, kv_ref[...]), energy)
     page = keep_ref.shape[0] // 2
     for slot, owner in ((0, member), (1, member ^ 2)):
         keep_ref[pl.ds(slot * page, page), :] = latent_ref[page_rows(pages_ref, owner, page), :]
@@ -231,7 +227,7 @@
     out_ref[:, KVR:] = turned[:, : columns - KVR].astype(BF16)
 
 
-def per_device(
+def layer(
     hidden_in,
     moe_gain,
     router_weight,
@@ -271,13 +267,14 @@
         return lax.all_to_all(blocks, "ep", 0, 0, tiled=True).reshape(slots, width)
 
     gain = moe_gain.reshape(1, full_width)
+    ids_t = expert_ids.T
     far_hidden = far(hidden_in)
     near_hidden = near(hidden_in)
     picked = call(
         functools.partial(pick_rows, groups),
         shape((slots, width), BF16),
         [VMEM] * 2,
-        expert_ids,
+        ids_t,
         hidden_in,
     )
     arrived = across(picked)
@@ -289,7 +286,7 @@
         local_scores,
         shape((16, rows), F32),
         [VMEM] * 4,
-        expert_ids,
+        ids_t,
         hidden_in,
         gain,
         router_weight,
@@ -297,11 +294,15 @@
     scores = scores + near(scores)
     far_scores = far(scores)
 
-    def whole_rows(name, a, b, c, d, w_gate, w_up, w_down):
+    def whole_rows(a, b, c, d, w_gate, w_up, w_down):
         count = a.shape[0]
         return call(
             feed_forward,
-            (shape((count, 2 * width), F32), shape((count, 2 * width), BF16)),
+            (
+                shape((count, width), F32),
+                shape((count, width), F32),
+                shape((count, 2 * width), BF16),
+            ),
             [VMEM] * 8,
             a,
             b,
@@ -314,30 +315,38 @@
             flops=6 * count * full_width * w_gate.shape[1],
         )
 
-    def halve(keep, send):
-        total = keep + near(send).astype(F32)
-        return total[:, :width], total[:, width:].astype(BF16)
-
-    shared_keep, shared_send = whole_rows(
-        "shared", hidden_in, near_hidden, far_hidden, diagonal_hidden,
+    def half(keep, got):
+        return (keep + got[:, width:].astype(F32)).astype(BF16)
+
+    shared_mine, shared_far, shared_send = whole_rows(
+        hidden_in, near_hidden, far_hidden, diagonal_hidden,
         shared_gate, shared_up, shared_down,
     )
-    shared_mine, shared_out = halve(shared_keep, shared_send)
+    shared_got = near(shared_send)
+    shared_out = half(shared_far, shared_got)
     shared_theirs = far(shared_out)
+    base = (
+        hidden_in.astype(F32)
+        + shared_mine
+        + shared_got[:, :width].astype(F32)
+        + shared_theirs.astype(F32)
+    )
 
     diagonal_rows = near(far_rows)
-    routed_keep, routed_send = whole_rows(
-        "routed", arrived, near_rows, far_rows, diagonal_rows,
+    routed_mine, routed_far, routed_send = whole_rows(
+        arrived, near_rows, far_rows, diagonal_rows,
         expert_gate[0], expert_up[0], expert_down[0],
     )
-    routed_mine, routed_out = halve(routed_keep, routed_send)
-    returned = across((routed_mine + far(routed_out).astype(F32)).astype(BF16))
+    routed_got = near(routed_send)
+    routed_theirs = far(half(routed_far, routed_got))
+    total = routed_mine + routed_got[:, :width].astype(F32) + routed_theirs.astype(F32)
+    returned = across(total.astype(BF16))
 
     gates = call(
         functools.partial(gate_matrix, groups, full_width),
         shape((rows, 2 * slots), BF16),
         [VMEM] * 3,
-        expert_ids,
+        ids_t,
         scores,
         far_scores,
     )
@@ -348,23 +357,21 @@
         doc_lengths,
         page_table,
     )
-    layer_out, latent_keep, latent_send, _ = call(
+    layer_out, latent_keep, latent_send = call(
         layer_end,
         (
             shape((rows, width), BF16),
             shape((2 * page, padded), F32),
             shape((2 * page, padded), BF16),
-            shape((rows, padded), F32),
         ),
-        [SMEM] + [VMEM] * 7,
+        [SMEM] + [VMEM] * 5,
         page_table,
         returned,
         gates,
-        hidden_in,
-        shared_mine,
-        shared_theirs,
+        base,
         attn_gain.reshape(1, width),
-        kv_down,
+        kv_down.T,
+        scratch=[pltpu.VMEM((rows, padded), F32)],
     )
     latent_mine, latent_out = call(
         functools.partial(latent_half, columns),
@@ -405,7 +412,7 @@
         P("ep", None),
     )
     return jax.shard_map(
-        per_device,
+        layer,
         mesh=mesh,
         in_specs=placed,
         out_specs=(P("ep", "tp"), P("ep", "tp", None, None)),

time: 89.2 us -> 72.4 us (0.81)
  Pallas kernels: 27.6 us -> 9.15 us
  waiting for transfers between devices: 22.5 us -> 27.8 us
  starting transfers between devices: 23.1 us -> 17.9 us
    pallas_call x9, Pallas kernels: 27.6 us -> 9.15 us  [call(): pl.pallas_call(body, out_shape=out_shape, in_specs=specs, out_specs=jax.t...]
    ppermute x6, waiting for transfers between devices: 11.5 us -> 17.6 us  [far(): return lax.ppermute(x, 'tp', [(i, i ^ 2) for i in range(members)])]
    unnamed x32 -> x44, local copies, waits for them, and re-layouts: 7.35 us -> 10.9 us
    all_to_all x2, starting transfers between devices: 13 us -> 10.2 us  [across(): return lax.all_to_all(blocks, 'ep', 0, 0, tiled=True).reshape(slots, width)]
    ppermute x6, starting transfers between devices: 8.98 us -> 6.71 us  [far(): return lax.ppermute(x, 'tp', [(i, i ^ 2) for i in range(members)])]
    slice x3 -> x0, local copies, waits for them, and re-layouts: 1.82 us -> none  [halve(): return (total[:, :width], total[:, width:].astype(BF16))]
    reshape x3, local copies, waits for them, and re-layouts: 3.19 us -> 1.97 us  [the longest x1 1.26 us: layer(): attn_gain.reshape(1, width)]
    convert_element_type x1 -> x3, other arithmetic: 0.75 us -> 1.74 us  [the longest x2 0.97 us: half(): return (keep + got[:, width:].astype(F32)).astype(BF16)]
  transfers between devices with their start and end apart: 16 -> 16, of which waited for: 9 -> 9; matrix products, arithmetic and copies ran while one was open for 10% -> 7% of each run, Pallas kernels for 20% -> 9%
where the time goes in v2:
time: 72.4 us; the launch traced here: 71.6 us
  waiting for transfers between devices  27.8 us (38%)
  starting transfers between devices  17.9 us (25%)
  local copies, waits for them, and re-layouts  12.9 us (18%)
  Pallas kernels  9.15 us (13%)
  other arithmetic  3.09 us (4%)
  between operations  0.87 us (1%)
    ppermute x6, waiting for transfers between devices, far(): return lax.ppermute(x, 'tp', [(i, i ^ 2) for i in range(members)])  17.6 us
    unnamed x44, local copies, waits for them, and re-layouts  10.9 us
    all_to_all x2, starting transfers between devices, across(): return lax.all_to_all(blocks, 'ep', 0, 0, tiled=True).reshape(slots, width)  10.2 us
    pallas_call x9, Pallas kernels, call(): pl.pallas_call(body, out_shape=out_shape, in_specs=specs, out_specs=jax.t...  9.15 us
    ppermute x6, starting transfers between devices, far(): return lax.ppermute(x, 'tp', [(i, i ^ 2) for i in range(members)])  6.71 us
    all_to_all x2, waiting for transfers between devices, across(): return lax.all_to_all(blocks, 'ep', 0, 0, tiled=True).reshape(slots, width)  6.04 us
    ppermute x8, waiting for transfers between devices, near(): return lax.ppermute(x, 'tp', [(i, i ^ 1) for i in range(members)])  4.17 us
  transfers between devices with their start and end apart: 16, of which 9 were waited for; matrix products, arithmetic and copies ran while one was open for 7% of the time, Pallas kernels for 9%

profile of v2, /device:TPU:0, one launch (start us, length us, event | category | flops | bytes accessed | tf_op | source)
XLA Modules:
  0.0 71.6 jit_solution(130597003050752916)
XLA Ops:
  0.6 3.1 %collective-permute-start.8 = (bf16[256,896]{1,0:T(8,128)(2,1)}, bf16[256,896]{1,0:T(8,128)(2,1)S(1)}, u32[]{:S(2)}, u32[]{:S(2)}) collective-permute-start(bf16[256,896]{1,0:T(8,128)(2,1)} %a_ref.1), channel_id=1, source_target_pairs={{0,2},{1,3},{2,0},{3,1},{4,6},{5,7},{6,4},{7,5},{8,10},{9,11},{10,... | collective-permute-start | bytes 1376264 | tf_op jit(solution)/shard_map/ppermute | solution.py:263
  3.7 1.1 %copy-done = bf16[256,896]{1,0:T(8,128)(2,1)S(1)} copy-done((bf16[256,896]{1,0:T(8,128)(2,1)S(1)}, bf16[256,896]{1,0:T(8,128)(2,1)}, u32[]{:S(2)}) %copy-start) | copy-done | bytes 458776
  4.7 0.7 copy-done.13
  5.4 1.1 %shard_map.158 = bf16[128,896]{1,0:T(8,128)(2,1)} custom-call(s32[8,256]{1,0:T(8,128)S(1)} %bitcast.18, bf16[256,896]{1,0:T(8,128)(2,1)S(1)} %copy-done), custom_call_target="tpu_custom_call" | custom-call | flops 1000000 | bytes 696320 | tf_op jit(solution)/shard_map/pallas_call | solution.py:28
  6.5 5.8 %all-to-all-start = ((bf16[8,16,896]{2,1,0:T(8,128)(2,1)}), bf16[8,16,896]{2,1,0:T(8,128)(2,1)S(1)}, u32[]{:S(2)}, u32[]{:S(2)}) async-start(bf16[8,16,896]{2,1,0:T(8,128)(2,1)} %bitcast.1), calls=%async_computation | async-start | bytes 458752 | tf_op jit(solution)/shard_map/all_to_all | solution.py:267
  12.3 0.0 collective-permute-start.7
  12.3 2.1 %collective-permute-done.8.c_ref = bf16[256,896]{1,0:T(8,128)(2,1)S(1)} collective-permute-done((bf16[256,896]{1,0:T(8,128)(2,1)}, bf16[256,896]{1,0:T(8,128)(2,1)S(1)}, u32[]{:S(2)}, u32[]{:S(2)}) %collective-permute-start.8) | collective-permute-done | bytes 458784 | tf_op jit(solution)/shard_map/ppermute | solution.py:263
  14.4 0.0 collective-permute-start.9
  14.4 6.0 %all-to-all-done = bf16[8,16,896]{2,1,0:T(8,128)(2,1)S(1)} async-done(((bf16[8,16,896]{2,1,0:T(8,128)(2,1)}), bf16[8,16,896]{2,1,0:T(8,128)(2,1)S(1)}, u32[]{:S(2)}, u32[]{:S(2)}) %all-to-all-start) | async-done | bytes 229408 | tf_op jit(solution)/shard_map/all_to_all | solution.py:267
  20.5 0.5 collective-permute-start.1
  21.0 0.7 reshape.30.gain_ref
  21.7 0.1 collective-permute-start
  21.8 4.7 %collective-permute-done.1.c_ref = bf16[128,896]{1,0:T(8,128)(2,1)S(1)} collective-permute-done((bf16[128,896]{1,0:T(8,128)(2,1)S(1)}, bf16[128,896]{1,0:T(8,128)(2,1)S(1)}, u32[]{:S(2)}, u32[]{:S(2)}) %collective-permute-start.1) | collective-permute-done | bytes 229408 | tf_op jit(solution)/shard_map/ppermute | solution.py:263
  26.5 0.0 collective-permute-start.2
  26.5 0.0 collective-permute-done.7.b_ref
  26.5 0.0 collective-permute-done.9.d_ref
  26.5 0.0 copy-start.1
  26.5 1.0 %copy-done.1 = bf16[256,896]{1,0:T(8,128)(2,1)S(1)} copy-done((bf16[256,896]{1,0:T(8,128)(2,1)S(1)}, bf16[256,896]{1,0:T(8,128)(2,1)}, u32[]{:S(2)}) %copy-start.1) | copy-done | bytes 458776
  27.5 1.5 %copy-done.3 = bf16[3584,256]{1,0:T(8,128)(2,1)S(1)} copy-done((bf16[3584,256]{1,0:T(8,128)(2,1)S(1)}, bf16[3584,256]{1,0:T(8,128)(2,1)}, u32[]{:S(2)}) %copy-start.3) | copy-done | bytes 1835032
  29.0 1.5 %copy-done.4 = bf16[3584,256]{1,0:T(8,128)(2,1)S(1)} copy-done((bf16[3584,256]{1,0:T(8,128)(2,1)S(1)}, bf16[3584,256]{1,0:T(8,128)(2,1)}, u32[]{:S(2)}) %copy-start.4) | copy-done | bytes 1835032
  30.5 1.5 %copy-done.5 = bf16[256,3584]{1,0:T(8,128)(2,1)S(1)} copy-done((bf16[256,3584]{1,0:T(8,128)(2,1)S(1)}, bf16[256,3584]{1,0:T(8,128)(2,1)}, u32[]{:S(2)}) %copy-start.5) | copy-done | bytes 1835032
  32.0 2.3 %shard_map.162 = (f32[256,896]{1,0:T(8,128)S(1)}, f32[256,896]{1,0:T(8,128)S(1)}, bf16[256,1792]{1,0:T(8,128)(2,1)S(1)}) custom-call(bf16[256,896]{1,0:T(8,128)(2,1)S(1)} %copy-done.1, bf16[256,896]{1,0:T(8,128)(2,1)S(1)} %collective-permute-done.7.b_ref, bf16[256,896]{1,0:T(8,128)(2,1)S(1)} %collective-permute-done.8.c_ref, ...), custom_call_target="tpu_custom_call" | custom-call | flops 1409286144 | bytes 10099712 | tf_op jit(solution)/shard_map/pallas_call | solution.py:28
  34.3 0.6 collective-permute-start.10
  34.9 0.0 collective-permute-done.b_ref
  34.9 0.0 collective-permute-done.2.d_ref
  34.9 1.3 %shard_map.159 = (f32[128,896]{1,0:T(8,128)S(1)}, f32[128,896]{1,0:T(8,128)S(1)}, bf16[128,1792]{1,0:T(8,128)(2,1)S(1)}) custom-call(bf16[128,896]{1,0:T(8,128)(2,1)S(1)} %bitcast.17, bf16[128,896]{1,0:T(8,128)(2,1)S(1)} %collective-permute-done.b_ref, bf16[128,896]{1,0:T(8,128)(2,1)S(1)} %collective-permute-done.1.c_ref, ...), custom_call_target="tpu_custom_call" | custom-call | flops 704643072 | bytes 7805952 | tf_op jit(solution)/shard_map/pallas_call | solution.py:28
  36.2 0.3 collective-permute-start.3
  36.5 1.6 %collective-permute-done.3 = bf16[128,1792]{1,0:T(8,128)(2,1)S(1)} collective-permute-done((bf16[128,1792]{1,0:T(8,128)(2,1)S(1)}, bf16[128,1792]{1,0:T(8,128)(2,1)S(1)}, u32[]{:S(2)}, u32[]{:S(2)}) %collective-permute-start.3) | collective-permute-done | bytes 458784 | tf_op jit(solution)/shard_map/ppermute | solution.py:260
  38.2 0.0 copy-start.2
  38.2 0.0 copy-start.12
  38.2 0.0 copy-start.14
  38.2 0.6 collective-permute-start.4
  38.8 0.0 collective-permute-done.10
  38.8 0.9 %add_convert_fusion = bf16[256,896]{1,0:T(8,128)(2,1)} fusion(f32[256,896]{1,0:T(8,128)S(1)} %get-tuple-element.20, bf16[256,1792]{1,0:T(8,128)(2,1)S(1)} %collective-permute-done.10), kind=kLoop, calls=%fused_computation.1 | loop fusion | flops 688128 | bytes 1835008 | tf_op jit(solution)/shard_map/convert_element_type | solution.py:319
  39.7 1.5 %collective-permute-start.11 = (bf16[256,896]{1,0:T(8,128)(2,1)}, bf16[256,896]{1,0:T(8,128)(2,1)}, u32[]{:S(2)}, u32[]{:S(2)}) collective-permute-start(bf16[256,896]{1,0:T(8,128)(2,1)} %add_convert_fusion), channel_id=1, source_target_pairs={{0,2},{1,3},{2,0},{3,1},{4,6},{5,7},{6,4},{7,5},{8,10},{9,11},{10,... | collective-permute-start | bytes 1376264 | tf_op jit(solution)/shard_map/ppermute | solution.py:263
  41.2 5.5 %collective-permute-done.4 = bf16[128,896]{1,0:T(8,128)(2,1)S(1)} collective-permute-done((bf16[128,896]{1,0:T(8,128)(2,1)S(1)}, bf16[128,896]{1,0:T(8,128)(2,1)S(1)}, u32[]{:S(2)}, u32[]{:S(2)}) %collective-permute-start.4) | collective-permute-done | bytes 229408 | tf_op jit(solution)/shard_map/ppermute | solution.py:263
  46.7 0.8 %add_convert_fusion.1 = bf16[128,896]{1,0:T(8,128)(2,1)} fusion(bf16[128,896]{1,0:T(8,128)(2,1)S(1)} %collective-permute-done.4, f32[128,896]{1,0:T(8,128)S(1)} %get-tuple-element.15, bf16[128,1792]{1,0:T(8,128)(2,1)S(1)} %collective-permute-done.3), kind=kLoop, calls=%fused_computation.2 | loop fusion | flops 573440 | bytes 1146880 | tf_op jit(solution)/shard_map/convert_element_type | solution.py:343
  47.5 4.4 %all-to-all-start.1 = ((bf16[8,16,896]{2,1,0:T(8,128)(2,1)}), bf16[8,16,896]{2,1,0:T(8,128)(2,1)S(1)}, u32[]{:S(2)}, u32[]{:S(2)}) async-start(bf16[8,16,896]{2,1,0:T(8,128)(2,1)} %bitcast.6), calls=%async_computation.1 | async-start | bytes 458752 | tf_op jit(solution)/shard_map/all_to_all | solution.py:267
  51.9 0.5 shard_map.160
  52.4 0.0 copy-start.9
  52.4 0.1 collective-permute-start.5
  52.5 1.2 %collective-permute-done.5 = f32[16,256]{1,0:T(8,128)S(1)} collective-permute-done((f32[16,256]{1,0:T(8,128)S(1)}, f32[16,256]{1,0:T(8,128)S(1)}, u32[]{:S(2)}, u32[]{:S(2)}) %collective-permute-start.5) | collective-permute-done | bytes 16416 | tf_op jit(solution)/shard_map/ppermute | solution.py:260
  53.7 0.5 collective-permute-start.6
  54.2 1.3 %reshape.33.gain_ref = bf16[1,896]{1,0:T(2,128)(2,1)} reshape(bf16[896]{0:T(1024)(128)(2,1)} %param.25) | data formatting | bytes 3584 | tf_op jit(solution)/shard_map/reshape | solution.py:372
  55.5 2.0 %collective-permute-done.6.theirs_ref = f32[16,256]{1,0:T(8,128)S(1)} collective-permute-done((f32[16,256]{1,0:T(8,128)S(1)}, f32[16,256]{1,0:T(8,128)S(1)}, u32[]{:S(2)}, u32[]{:S(2)}) %collective-permute-start.6) | collective-permute-done | bytes 16416 | tf_op jit(solution)/shard_map/ppermute | solution.py:263
  57.4 0.7 copy-done.15
  58.1 0.3 shard_map.161.gates_ref
  58.4 0.6 copy-done.10
  59.1 1.3 %convert_add_fusion.base_ref = f32[256,896]{1,0:T(8,128)S(1)} fusion(bf16[256,896]{1,0:T(8,128)(2,1)} %collective-permute-done.11, f32[256,896]{1,0:T(8,128)S(1)} %get-tuple-element.18, bf16[256,896]{1,0:T(8,128)(2,1)S(1)} %copy-done.2, bf16[256,1792]{1,0:T(8,128)(2,1)} %copy-done.20), kind=kLoop, calls=%fused_computation | loop fusion | flops 1376256 | bytes 3211264 | tf_op jit(solution)/shard_map/add | solution.py:329
  60.4 0.0 copy-start.21
  60.4 0.0 copy-start.18
  60.4 0.0 copy-start.19
  60.4 0.0 all-to-all-done.1
  60.5 0.9 %copy-done.11 = bf16[256,256]{1,0:T(8,128)(2,1)S(1)} copy-done((bf16[256,256]{1,0:T(8,128)(2,1)S(1)}, bf16[256,256]{1,0:T(8,128)(2,1)}, u32[]{:S(2)}) %copy-start.11) | copy-done | bytes 131096
  61.4 0.7 copy-done.16
  62.0 0.7 copy-done.17
  62.7 1.9 %shard_map.163 = (bf16[256,896]{1,0:T(8,128)(2,1)}, f32[128,640]{1,0:T(8,128)S(1)}, bf16[128,640]{1,0:T(8,128)(2,1)S(1)}) custom-call(s32[1,4]{1,0:T(1,128)S(1)} %copy-done.17, bf16[128,896]{1,0:T(8,128)(2,1)S(1)} %bitcast.14, bf16[256,256]{1,0:T(8,128)(2,1)S(1)} %copy-done.11, f32[256,896]{1,0:T(8,128)S(1)} %convert_add_fusion.base_ref, ...), custom_call_target="tpu_custom_call" | custom-call | flops 1000000 | bytes 3262224 | tf_op jit(solution)/shard_map/pallas_call | solution.py:28
  64.6 0.0 collective-permute-start.12
  64.6 1.4 %collective-permute-done.12.got_ref = bf16[128,640]{1,0:T(8,128)(2,1)S(1)} collective-permute-done((bf16[128,640]{1,0:T(8,128)(2,1)S(1)}, bf16[128,640]{1,0:T(8,128)(2,1)S(1)}, u32[]{:S(2)}, u32[]{:S(2)}) %collective-permute-start.12) | collective-permute-done | bytes 163872 | tf_op jit(solution)/shard_map/ppermute | solution.py:260
  65.9 0.2 shard_map.164
  66.2 0.5 collective-permute-start.13
  66.8 0.7 shard_map.165
  67.5 3.3 %collective-permute-done.13.got_ref = bf16[64,640]{1,0:T(8,128)(2,1)S(1)} collective-permute-done((bf16[64,640]{1,0:T(8,128)(2,1)S(1)}, bf16[64,640]{1,0:T(8,128)(2,1)S(1)}, u32[]{:S(2)}, u32[]{:S(2)}) %collective-permute-start.13) | collective-permute-done | bytes 81952 | tf_op jit(solution)/shard_map/ppermute | solution.py:263
  70.7 0.9 %shard_map.166 = bf16[64,576]{1,0:T(8,128)(2,1)} custom-call(f32[64,640]{1,0:T(8,128)S(1)} %get-tuple-element.24.mine_ref, bf16[64,640]{1,0:T(8,128)(2,1)S(1)} %collective-permute-done.13.got_ref, bf16[1,512]{1,0:T(2,128)(2,1)S(1)} %reshape.34.gain_ref, f32[64,128]{1,0:T(8,128)S(1)} %get-tuple-element.26.cos_ref, f32[64,128]{1,0:T(8,128)S(1)} %get-tuple-element.27.sin_ref), custom_call_target="tpu_custom_call" | custom-call | flops 1000000 | bytes 386048 | tf_op jit(solution)/shard_map/pallas_call | solution.py:28
  (29 shorter events, 0.1 us)
Async XLA Ops:
  0.6 13.8 %collective-permute-start.8 = (bf16[256,896]{1,0:T(8,128)(2,1)}, bf16[256,896]{1,0:T(8,128)(2,1)S(1)}, u32[]{:S(2)}, u32[]{:S(2)}) collective-permute-start(bf16[256,896]{1,0:T(8,128)(2,1)} %a_ref.1), channel_id=1, source_target_pairs={{0,2},{1,3},{2,0},{3,1},{4,6},{5,7},{6,4},{7,5},{8,10},{9,11},{10,... | collective-permute-start | bytes 1376264 | tf_op jit(solution)/shard_map/ppermute | solution.py:263
  3.7 1.1 %copy-start = (bf16[256,896]{1,0:T(8,128)(2,1)S(1)}, bf16[256,896]{1,0:T(8,128)(2,1)}, u32[]{:S(2)}) copy-start(bf16[256,896]{1,0:T(8,128)(2,1)} %a_ref.1) | copy-start | bytes 1376260
  4.7 0.7 copy-start.13
  6.5 14.0 %all-to-all-start = ((bf16[8,16,896]{2,1,0:T(8,128)(2,1)}), bf16[8,16,896]{2,1,0:T(8,128)(2,1)S(1)}, u32[]{:S(2)}, u32[]{:S(2)}) async-start(bf16[8,16,896]{2,1,0:T(8,128)(2,1)} %bitcast.1), calls=%async_computation | async-start | bytes 458752 | tf_op jit(solution)/shard_map/all_to_all | solution.py:267
  12.3 14.2 %collective-permute-start.7 = (bf16[256,896]{1,0:T(8,128)(2,1)}, bf16[256,896]{1,0:T(8,128)(2,1)S(1)}, u32[]{:S(2)}, u32[]{:S(2)}) collective-permute-start(bf16[256,896]{1,0:T(8,128)(2,1)} %a_ref.1), channel_id=1, source_target_pairs={{0,1},{1,0},{2,3},{3,2},{4,5},{5,4},{6,7},{7,6},{8,9},{9,8},{10,11... | collective-permute-start | bytes 1376264 | tf_op jit(solution)/shard_map/ppermute | solution.py:260
  14.4 12.1 %collective-permute-start.9 = (bf16[256,896]{1,0:T(8,128)(2,1)S(1)}, bf16[256,896]{1,0:T(8,128)(2,1)S(1)}, u32[]{:S(2)}, u32[]{:S(2)}) collective-permute-start(bf16[256,896]{1,0:T(8,128)(2,1)S(1)} %collective-permute-done.8.c_ref), channel_id=1, source_target_pairs={{0,1},{1,0},{2,3},{3,2},{4,5},{5,4},{6,7},{7,6},{8,9},{9,8},{10,11... | collective-permute-start | bytes 1376264 | tf_op jit(solution)/shard_map/ppermute | solution.py:260
  20.5 6.0 %collective-permute-start.1 = (bf16[128,896]{1,0:T(8,128)(2,1)S(1)}, bf16[128,896]{1,0:T(8,128)(2,1)S(1)}, u32[]{:S(2)}, u32[]{:S(2)}) collective-permute-start(bf16[128,896]{1,0:T(8,128)(2,1)S(1)} %bitcast.15), channel_id=1, source_target_pairs={{0,2},{1,3},{2,0},{3,1},{4,6},{5,7},{6,4},{7,5},{8,10},{9,11},{10,... | collective-permute-start | bytes 688136 | tf_op jit(solution)/shard_map/ppermute | solution.py:263
  21.7 13.2 %collective-permute-start = (bf16[128,896]{1,0:T(8,128)(2,1)S(1)}, bf16[128,896]{1,0:T(8,128)(2,1)S(1)}, u32[]{:S(2)}, u32[]{:S(2)}) collective-permute-start(bf16[128,896]{1,0:T(8,128)(2,1)S(1)} %bitcast.16), channel_id=1, source_target_pairs={{0,1},{1,0},{2,3},{3,2},{4,5},{5,4},{6,7},{7,6},{8,9},{9,8},{10,11... | collective-permute-start | bytes 688136 | tf_op jit(solution)/shard_map/ppermute | solution.py:260
  26.5 8.4 %collective-permute-start.2 = (bf16[128,896]{1,0:T(8,128)(2,1)S(1)}, bf16[128,896]{1,0:T(8,128)(2,1)S(1)}, u32[]{:S(2)}, u32[]{:S(2)}) collective-permute-start(bf16[128,896]{1,0:T(8,128)(2,1)S(1)} %collective-permute-done.1.c_ref), channel_id=1, source_target_pairs={{0,1},{1,0},{2,3},{3,2},{4,5},{5,4},{6,7},{7,6},{8,9},{9,8},{10,11... | collective-permute-start | bytes 688136 | tf_op jit(solution)/shard_map/ppermute | solution.py:260
  26.5 1.0 %copy-start.1 = (bf16[256,896]{1,0:T(8,128)(2,1)S(1)}, bf16[256,896]{1,0:T(8,128)(2,1)}, u32[]{:S(2)}) copy-start(bf16[256,896]{1,0:T(8,128)(2,1)} %a_ref.1) | copy-start | bytes 1376260
  27.5 1.5 %copy-start.3 = (bf16[3584,256]{1,0:T(8,128)(2,1)S(1)}, bf16[3584,256]{1,0:T(8,128)(2,1)}, u32[]{:S(2)}) copy-start(bf16[3584,256]{1,0:T(8,128)(2,1)} %gate_ref.1) | copy-start | bytes 5505028
  29.0 1.5 %copy-start.4 = (bf16[3584,256]{1,0:T(8,128)(2,1)S(1)}, bf16[3584,256]{1,0:T(8,128)(2,1)}, u32[]{:S(2)}) copy-start(bf16[3584,256]{1,0:T(8,128)(2,1)} %up_ref.1) | copy-start | bytes 5505028
  30.5 1.5 %copy-start.5 = (bf16[256,3584]{1,0:T(8,128)(2,1)S(1)}, bf16[256,3584]{1,0:T(8,128)(2,1)}, u32[]{:S(2)}) copy-start(bf16[256,3584]{1,0:T(8,128)(2,1)} %down_ref.1) | copy-start | bytes 5505028
  32.0 2.9 %copy-start.6 = (bf16[1,3584,256]{2,1,0:T(8,128)(2,1)S(1)}, bf16[1,3584,256]{2,1,0:T(8,128)(2,1)}, u32[]{:S(2)}) copy-start(bf16[1,3584,256]{2,1,0:T(8,128)(2,1)} %param.22) | copy-start | bytes 5505028
  32.0 2.9 %copy-start.7 = (bf16[1,3584,256]{2,1,0:T(8,128)(2,1)S(1)}, bf16[1,3584,256]{2,1,0:T(8,128)(2,1)}, u32[]{:S(2)}) copy-start(bf16[1,3584,256]{2,1,0:T(8,128)(2,1)} %param.23) | copy-start | bytes 5505028
  32.0 2.9 %copy-start.8 = (bf16[1,256,3584]{2,1,0:T(8,128)(2,1)S(1)}, bf16[1,256,3584]{2,1,0:T(8,128)(2,1)}, u32[]{:S(2)}) copy-start(bf16[1,256,3584]{2,1,0:T(8,128)(2,1)} %param.24) | copy-start | bytes 5505028
  34.3 4.5 %collective-permute-start.10 = (bf16[256,1792]{1,0:T(8,128)(2,1)S(1)}, bf16[256,1792]{1,0:T(8,128)(2,1)S(1)}, u32[]{:S(2)}, u32[]{:S(2)}) collective-permute-start(bf16[256,1792]{1,0:T(8,128)(2,1)S(1)} %get-tuple-element.19), channel_id=1, source_target_pairs={{0,1},{1,0},{2,3},{3,2},{4,5},{5,4},{6,7},{7,6},{8,9},{9,8},{10,11... | collective-permute-start | bytes 2752520 | tf_op jit(solution)/shard_map/ppermute | solution.py:260
  36.2 1.9 %collective-permute-start.3 = (bf16[128,1792]{1,0:T(8,128)(2,1)S(1)}, bf16[128,1792]{1,0:T(8,128)(2,1)S(1)}, u32[]{:S(2)}, u32[]{:S(2)}) collective-permute-start(bf16[128,1792]{1,0:T(8,128)(2,1)S(1)} %get-tuple-element.16), channel_id=1, source_target_pairs={{0,1},{1,0},{2,3},{3,2},{4,5},{5,4},{6,7},{7,6},{8,9},{9,8},{10,11... | collective-permute-start | bytes 1376264 | tf_op jit(solution)/shard_map/ppermute | solution.py:260
  38.2 13.7 %copy-start.2 = (bf16[256,896]{1,0:T(8,128)(2,1)S(1)}, bf16[256,896]{1,0:T(8,128)(2,1)}, u32[]{:S(2)}) copy-start(bf16[256,896]{1,0:T(8,128)(2,1)} %a_ref.1) | copy-start | bytes 1376260
  38.2 13.7 %copy-start.12 = (bf16[896,256]{1,0:T(8,128)(2,1)S(1)}, bf16[896,256]{1,0:T(8,128)(2,1)}, u32[]{:S(2)}) copy-start(bf16[896,256]{1,0:T(8,128)(2,1)} %router_ref.1) | copy-start | bytes 1376260
  38.2 13.7 %copy-start.14 = (s32[256,8]{0,1:T(8,128)S(1)}, s32[256,8]{0,1:T(8,128)}, u32[]{:S(2)}) copy-start(s32[256,8]{0,1:T(8,128)} %param.18) | copy-start | bytes 24580
  38.2 8.5 %collective-permute-start.4 = (bf16[128,896]{1,0:T(8,128)(2,1)S(1)}, bf16[128,896]{1,0:T(8,128)(2,1)S(1)}, u32[]{:S(2)}, u32[]{:S(2)}) collective-permute-start(bf16[128,896]{1,0:T(8,128)(2,1)S(1)} %add_convert_fusion.2), channel_id=1, source_target_pairs={{0,2},{1,3},{2,0},{3,1},{4,6},{5,7},{6,4},{7,5},{8,10},{9,11},{10,... | collective-permute-start | bytes 688136 | tf_op jit(solution)/shard_map/ppermute | solution.py:263
  38.8 8.7 %copy-start.20 = (bf16[256,1792]{1,0:T(8,128)(2,1)}, bf16[256,1792]{1,0:T(8,128)(2,1)S(1)}, u32[]{:S(2)}) copy-start(bf16[256,1792]{1,0:T(8,128)(2,1)S(1)} %collective-permute-done.10) | copy-start | bytes 2752516
  39.7 19.3 %collective-permute-start.11 = (bf16[256,896]{1,0:T(8,128)(2,1)}, bf16[256,896]{1,0:T(8,128)(2,1)}, u32[]{:S(2)}, u32[]{:S(2)}) collective-permute-start(bf16[256,896]{1,0:T(8,128)(2,1)} %add_convert_fusion), channel_id=1, source_target_pairs={{0,2},{1,3},{2,0},{3,1},{4,6},{5,7},{6,4},{7,5},{8,10},{9,11},{10,... | collective-permute-start | bytes 1376264 | tf_op jit(solution)/shard_map/ppermute | solution.py:263
  47.5 12.9 %all-to-all-start.1 = ((bf16[8,16,896]{2,1,0:T(8,128)(2,1)}), bf16[8,16,896]{2,1,0:T(8,128)(2,1)S(1)}, u32[]{:S(2)}, u32[]{:S(2)}) async-start(bf16[8,16,896]{2,1,0:T(8,128)(2,1)} %bitcast.6), calls=%async_computation.1 | async-start | bytes 458752 | tf_op jit(solution)/shard_map/all_to_all | solution.py:267
  52.4 8.0 %copy-start.9 = (bf16[896,576]{0,1:T(8,128)(2,1)S(1)}, bf16[896,576]{0,1:T(8,128)(2,1)}, u32[]{:S(2)}) copy-start(bf16[896,576]{0,1:T(8,128)(2,1)} %param.26) | copy-start | bytes 3096580
  52.4 1.2 %collective-permute-start.5 = (f32[16,256]{1,0:T(8,128)S(1)}, f32[16,256]{1,0:T(8,128)S(1)}, u32[]{:S(2)}, u32[]{:S(2)}) collective-permute-start(f32[16,256]{1,0:T(8,128)S(1)} %shard_map.160), channel_id=1, source_target_pairs={{0,1},{1,0},{2,3},{3,2},{4,5},{5,4},{6,7},{7,6},{8,9},{9,8},{10,11... | collective-permute-start | bytes 49160 | tf_op jit(solution)/shard_map/ppermute | solution.py:260
  53.7 3.7 %collective-permute-start.6 = (f32[16,256]{1,0:T(8,128)S(1)}, f32[16,256]{1,0:T(8,128)S(1)}, u32[]{:S(2)}, u32[]{:S(2)}) collective-permute-start(f32[16,256]{1,0:T(8,128)S(1)} %add.27.mine_ref), channel_id=1, source_target_pairs={{0,2},{1,3},{2,0},{3,1},{4,6},{5,7},{6,4},{7,5},{8,10},{9,11},{10,... | collective-permute-start | bytes 49160 | tf_op jit(solution)/shard_map/ppermute | solution.py:263
  57.4 0.7 copy-start.15
  58.4 0.6 copy-start.10
  60.4 6.3 %copy-start.21 = (bf16[512]{0:T(512)(128)(2,1)S(1)}, bf16[512]{0:T(512)(128)(2,1)}, u32[]{:S(2)}) copy-start(bf16[512]{0:T(512)(128)(2,1)} %param.27) | copy-start | bytes 3076
  60.4 6.3 %copy-start.18 = (s32[1,4]{1,0:T(1,128)S(1)}, s32[1,4]{1,0:T(1,128)}, u32[]{:S(2)}) copy-start(s32[1,4]{1,0:T(1,128)} %pages_ref.3) | copy-start | bytes 52
  60.4 6.3 %copy-start.19 = (s32[1,4]{1,0:T(1,128)S(1)}, s32[1,4]{1,0:T(1,128)}, u32[]{:S(2)}) copy-start(s32[1,4]{1,0:T(1,128)} %lengths_ref.1) | copy-start | bytes 52
  60.5 0.9 %copy-start.11 = (bf16[256,256]{1,0:T(8,128)(2,1)S(1)}, bf16[256,256]{1,0:T(8,128)(2,1)}, u32[]{:S(2)}) copy-start(bf16[256,256]{1,0:T(8,128)(2,1)} %copy-done.10) | copy-start | bytes 393220
  61.4 0.7 copy-start.16
  62.0 0.7 copy-start.17
  64.6 1.4 %collective-permute-start.12 = (bf16[128,640]{1,0:T(8,128)(2,1)S(1)}, bf16[128,640]{1,0:T(8,128)(2,1)S(1)}, u32[]{:S(2)}, u32[]{:S(2)}) collective-permute-start(bf16[128,640]{1,0:T(8,128)(2,1)S(1)} %get-tuple-element.23), channel_id=1, source_target_pairs={{0,1},{1,0},{2,3},{3,2},{4,5},{5,4},{6,7},{7,6},{8,9},{9,8},{10,11... | collective-permute-start | bytes 491528 | tf_op jit(solution)/shard_map/ppermute | solution.py:260
  66.2 4.5 %collective-permute-start.13 = (bf16[64,640]{1,0:T(8,128)(2,1)S(1)}, bf16[64,640]{1,0:T(8,128)(2,1)S(1)}, u32[]{:S(2)}, u32[]{:S(2)}) collective-permute-start(bf16[64,640]{1,0:T(8,128)(2,1)S(1)} %get-tuple-element.25), channel_id=1, source_target_pairs={{0,2},{1,3},{2,0},{3,1},{4,6},{5,7},{6,4},{7,5},{8,10},{9,11},{10,... | collective-permute-start | bytes 245768 | tf_op jit(solution)/shard_map/ppermute | solution.py:263
